TPU v7x, 32 devices: a whole 2x2x4 slice. The times are simulated.
32 devices in a mesh: gx: 4 (over z), gy: 8 (over y, x, core).
Axes of the slice: x: 2, y: 2, z: 4, core: 2. Of those that a mesh axis runs over, the one named last changes fastest.
Arguments:
- state_field: float32 [32, 32, 2048], P(None, 'gx', 'gy'), may hold values from -6 to 6
- spectral_weight: float32 [32, 32, 2, 32, 512], P('gx', 'gy'), may hold values from -6 to 6
- conv_fine: float32 [27, 32, 32], replicated, may hold values from -0.21875 to 0.21875
- conv_coarse: float32 [27, 32, 32], replicated, may hold values from -0.21875 to 0.21875
- conv_mix: float32 [32, 32], replicated, may hold values from -1 to 1
- linear_weight: float32 [32, 32], replicated, may hold values from -1 to 1
- bias_vector: float32 [32], replicated, may hold values from -3 to 3
Outputs:
- layer_out: float32 [32, 32, 2048], P(None, 'gx', 'gy')
All inputs are finite; a program needn't handle non-finite values.
Results may differ from a plain program's by a relative error of at most 0.0001.
Values sent between devices are 32-bit elements; how exact they have to be, the bound alone decides.
A program may use at most 64 MiB of HBM per device.

v0:
```python
import functools
import math

import jax
import jax.numpy as jnp
import numpy as np
from jax import lax
from jax.experimental import pallas as pl
from jax.experimental.pallas import tpu as pltpu
from jax.sharding import PartitionSpec as P

KX = 32
KY = 32
KZ = 16
NZ = 32


exact_precision = lax.Precision.HIGH


def extended(cells, sides, width):
    for axis, dim in sides:
        count = lax.axis_size(axis)
        ends = count - 1
        head = lax.slice_in_dim(cells, 0, width, axis=dim)
        tail = lax.slice_in_dim(cells, cells.shape[dim] - width, cells.shape[dim], axis=dim)
        cells = jnp.concatenate(
            [
                lax.ppermute(tail, axis, [(i, (i + 1) % count) for i in range(ends)]),
                cells,
                lax.ppermute(head, axis, [((i + 1) % count, i) for i in range(ends)]),
            ],
            axis=dim,
        )
    return cells


def mode_frequency(count, length):
    indices = jnp.arange(count, dtype=jnp.int32)
    return jnp.where(indices < count // 2, indices, indices - count + length)


def forward_table(count, length, start, cells):
    frequency = mode_frequency(count, length)
    places = start + jnp.arange(cells, dtype=jnp.int32)
    phase = frequency[:, None] * places[None, :] % length
    angles = phase.astype(jnp.float32) * (2.0 * math.pi / length)
    cosines = jnp.cos(angles)
    sines = jnp.sin(angles)
    upper_rows = jnp.stack([cosines, sines], axis=-1)
    lower_rows = jnp.stack([-sines, cosines], axis=-1)
    return jnp.stack([upper_rows, lower_rows], axis=1)


def conv_merged(padded, weight, cells_x, cells_y, depth):
    channels = padded.shape[0]
    flat = padded.reshape(channels, cells_x + 2, (cells_y + 2) * depth)
    flat = jnp.pad(flat, ((0, 0), (0, 0), (1, 1)))
    width = cells_y * depth
    positions = jnp.arange(width, dtype=jnp.int32) % depth
    lower_keep = (positions > 0).astype(jnp.float32)
    upper_keep = (positions < depth - 1).astype(jnp.float32)
    accumulated = jnp.zeros((channels, cells_x, width), jnp.float32)
    for offset in range(27):
        shift_x, shift_y, shift_z = (offset // 9, offset // 3 % 3, offset % 3)
        start = shift_y * depth + shift_z
        window = flat[:, shift_x : shift_x + cells_x, start : start + width]
        term = jnp.einsum("oi,ixw->oxw", weight[offset], window, precision=exact_precision)
        if shift_z == 0:
            term = term * lower_keep
        elif shift_z == 2:
            term = term * upper_keep
        accumulated = accumulated + term
    return accumulated


def contract(values, kernel):
    return jnp.einsum("xyiz,xyioz->xyoz", values, kernel, precision=exact_precision)


def mix_modes(owned_modes, spectral_weight, channels):
    rows_x, rows_y = (owned_modes.shape[0], owned_modes.shape[1])
    values = owned_modes.reshape(rows_x, rows_y, 2, channels, KZ)
    kernel = spectral_weight.reshape(rows_x, rows_y, 2, channels, channels, KZ)
    real_part = contract(values[:, :, 0], kernel[:, :, 0]) - contract(
        values[:, :, 1], kernel[:, :, 1]
    )
    imag_part = contract(values[:, :, 0], kernel[:, :, 1]) + contract(
        values[:, :, 1], kernel[:, :, 0]
    )
    return jnp.stack([real_part, imag_part], axis=2).reshape(rows_x, rows_y, 2, channels * KZ)


MESH = pl.DeviceIdType.MESH


def split_pair(values):
    high = values.astype(jnp.bfloat16)
    return high, (values - high.astype(jnp.float32)).astype(jnp.bfloat16)


def dot_split(left, high, low):
    left_high, left_low = split_pair(left)
    dot = functools.partial(jnp.dot, preferred_element_type=jnp.float32)
    return dot(left_high, high) + dot(left_high, low) + dot(left_low, high)


def host_pair(values):
    high = values.astype(np.float32).astype(jnp.bfloat16)
    low = (values - high.astype(np.float64)).astype(np.float32).astype(jnp.bfloat16)
    return jnp.asarray(high), jnp.asarray(low)


def host_frequency(count, length):
    indices = np.arange(count)
    return np.where(indices < count // 2, indices, indices - count + length)


def spectral_tables(groups_x, groups_y, cells_x, cells_y, rows_y):
    total_x, total_y = groups_x * cells_x, groups_y * cells_y
    fy = host_frequency(KY, total_y)
    places = np.arange(cells_y)
    kz = np.arange(KZ)
    zs = np.arange(NZ)
    turn_y = places[:, None] * fy[None, :] % total_y / total_y
    turn_z = zs[:, None] * kz[None, :] % NZ / NZ
    angle = 2 * np.pi * (turn_y[:, None, :, None] + turn_z[None, :, None, :])
    table = np.stack([np.cos(angle), -np.sin(angle)], axis=2)
    table = table.reshape(cells_y * NZ, 2, groups_y, rows_y, KZ).transpose(2, 0, 1, 3, 4)
    table = table.reshape(groups_y, cells_y * NZ, 2 * rows_y * KZ)
    scale = np.tile(np.where(kz == 0, 1.0, 2.0) / (total_x * total_y * NZ), 2 * rows_y)
    inverse = (table * scale).transpose(0, 2, 1)
    starts = np.arange(groups_y) * cells_y
    phase = 2 * np.pi * (starts[:, None] * fy[None, :] % total_y) / total_y
    phase = np.broadcast_to(phase.reshape(-1, 1, rows_y, 1), (groups_y**2, 2, rows_y, KZ))
    signs = np.array([1.0, -1.0]).reshape(1, 2, 1, 1)
    rotation = np.stack([np.cos(phase), signs * np.sin(phase)], axis=1)
    rotation = rotation.reshape(groups_y**2, 2, 2 * rows_y * KZ).astype(np.float32)
    fx = host_frequency(KX, total_x)
    angle_x = 2 * np.pi * (fx[:, None] * np.arange(total_x)[None, :] % total_x) / total_x
    table_x = np.stack([np.cos(angle_x), np.sin(angle_x)]).reshape(-1).astype(np.float32)
    return (*host_pair(table), *host_pair(inverse), jnp.asarray(rotation), jnp.asarray(table_x))


def lane_group(shape, axis, width):
    return lax.broadcasted_iota(jnp.int32, shape, axis) // width


def spectral_kernel(
    groups_x, groups_y, cells_x, rows_x, rows_y, channels,
    cells_ref, fwd_high, fwd_low, inv_high, inv_low, rotation, table_x, weight_hbm,
    out_ref,
    parts, parts_in, line, line_in, mixed, mixed_in, back, back_in, weight,
    send_sem, recv_sem, weight_sem,
):
    mx, my = lax.axis_index("gx"), lax.axis_index("gy")
    lanes = 2 * rows_y * KZ
    groups = 2 * rows_y
    total_x = groups_x * cells_x
    load_weight = pltpu.make_async_copy(weight_hbm, weight, weight_sem)
    load_weight.start()
    barrier = pltpu.get_barrier_semaphore()
    for step in range(1, groups_y):
        pl.semaphore_signal(
            barrier, inc=1, device_id=(mx, lax.rem(my + step, groups_y)), device_id_type=MESH
        )
    for step in range(1, groups_x):
        pl.semaphore_signal(
            barrier, inc=1, device_id=(lax.rem(mx + step, groups_x), my), device_id_type=MESH
        )
    pl.semaphore_wait(barrier, groups_x + groups_y - 2)

    def send(phase, step, source, target, device):
        copy = pltpu.make_async_remote_copy(
            src_ref=source, dst_ref=target,
            send_sem=send_sem.at[phase, step], recv_sem=recv_sem.at[phase, step],
            device_id=device, device_id_type=MESH,
        )
        copy.start()
        return copy

    half = lanes // 2
    left_high, left_low = split_pair(cells_ref[...])
    dot = functools.partial(jnp.dot, preferred_element_type=jnp.float32)
    copies = []
    for step in list(range(1, groups_y)) + [0]:
        peer = lax.rem(my + step, groups_y)
        high, low = fwd_high[peer], fwd_low[peer]
        part = dot(left_high, high) + dot(left_high, low) + dot(left_low, high)
        turn = rotation[my * groups_y + peer]
        part = part * turn[0:1] + pltpu.roll(part, half, 1) * turn[1:2]
        parts[step] = part
        if step:
            copies.append(send(0, step, parts.at[step], parts_in.at[step], (mx, peer)))
    total = parts[0]
    for step, copy in enumerate(copies, 1):
        copy.wait()
        total = total + parts_in[step]
    line[...] = total
    copies = [
        send(1, step, line, line_in.at[step], (lax.rem(mx + step, groups_x), my))
        for step in range(1, groups_x)
    ]
    for copy in copies:
        copy.wait()
    load_weight.wait()
    lane = lax.broadcasted_iota(jnp.int32, (channels, lanes), 1)
    sign = jnp.where(lane < half, 1.0, -1.0).astype(jnp.float32)
    group = lane // KZ
    row_8 = lax.broadcasted_iota(jnp.int32, (groups, lanes), 0)
    diagonal = lax.rem(row_8 - lax.broadcasted_iota(jnp.int32, (groups, lanes), 1) // KZ + groups, groups)

    def spread(values, index):
        picked = jnp.where(group == index, values, 0.0)
        shift = KZ
        while shift < lanes:
            picked = picked + pltpu.roll(picked, shift, 1)
            shift *= 2
        return picked

    def along_x(own, others, rows, place):
        first = jnp.zeros((channels, lanes), jnp.float32)
        second = jnp.zeros((channels, lanes), jnp.float32)
        for step in range(groups_x):
            base = lax.rem(mx - step + groups_x, groups_x) * rows
            for row in range(rows):
                position = place(base + row)
                block = pl.ds(row * channels, channels)
                values = own[block, :] if step == 0 else others[step, block, :]
                first = first + values * table_x[position]
                second = second + values * table_x[KX * total_x + position]
        return first, pltpu.roll(second, half, 1) * sign

    def one_mode(j, carry):
        first, second = along_x(line, line_in, cells_x, lambda x: (mx * rows_x + j) * total_x + x)
        modes = first + second
        tiles = channels * KZ // lanes
        rows = [jnp.zeros((groups, lanes), jnp.float32) for _ in range(tiles)]
        for k in range(rows_y):
            real, imag = spread(modes, k), spread(modes, rows_y + k)
            for tile in range(tiles):
                columns = pl.ds(tile * lanes, lanes)
                w_real = weight[j, k, 0, :, columns]
                w_imag = weight[j, k, 1, :, columns]
                out_real = jnp.sum(real * w_real - imag * w_imag, axis=0, keepdims=True)
                out_imag = jnp.sum(real * w_imag + imag * w_real, axis=0, keepdims=True)
                rows[tile] = jnp.where(row_8 == k, out_real, rows[tile])
                rows[tile] = jnp.where(row_8 == rows_y + k, out_imag, rows[tile])
        for tile in range(tiles):
            turned = jnp.where(diagonal == 0, rows[tile], 0.0)
            for d in range(1, groups):
                moved = pltpu.roll(pltpu.roll(rows[tile], d, 0), lanes - KZ * d, 1)
                turned = jnp.where(diagonal == d, moved, turned)
            start = pl.multiple_of(j * channels + tile * groups, groups)
            mixed[pl.ds(start, groups), :] = turned
        return carry

    lax.fori_loop(0, rows_x, one_mode, 0)
    copies = [
        send(2, step, mixed, mixed_in.at[step], (lax.rem(mx + step, groups_x), my))
        for step in range(1, groups_x)
    ]
    for copy in copies:
        copy.wait()

    def one_line(j, carry):
        first, second = along_x(mixed, mixed_in, rows_x, lambda k: k * total_x + mx * cells_x + j)
        back[pl.ds(pl.multiple_of(j * channels, channels), channels), :] = first - second
        return carry

    lax.fori_loop(0, cells_x, one_line, 0)
    copies = [
        send(3, step, back, back_in.at[step], (mx, lax.rem(my + step, groups_y)))
        for step in range(1, groups_y)
    ]
    result = None
    for step in range(groups_y):
        if step:
            copies[step - 1].wait()
        values = back_in[step] if step else back[...]
        peer = lax.rem(my - step + groups_y, groups_y)
        turn = rotation[my * groups_y + peer]
        values = values * turn[0:1] - pltpu.roll(values, half, 1) * turn[1:2]
        term = dot_split(values, inv_high[peer], inv_low[peer])
        result = term if result is None else result + term
    out_ref[...] = result


def spectral(cells, spectral_weight, cells_y):
    cells_x, channels, plane = cells.shape
    rows_x, rows_y = spectral_weight.shape[:2]
    groups_x, groups_y = lax.axis_size("gx"), lax.axis_size("gy")
    lanes = 2 * rows_y * KZ
    tables = spectral_tables(groups_x, groups_y, cells_x, cells_y, rows_y)
    slab_x, slab_k = (cells_x * channels, lanes), (rows_x * channels, lanes)
    f32 = jnp.float32
    vmem = pl.BlockSpec(memory_space=pltpu.VMEM)
    return pl.pallas_call(
        functools.partial(
            spectral_kernel, groups_x, groups_y, cells_x, rows_x, rows_y, channels
        ),
        out_shape=jax.ShapeDtypeStruct((cells_x * channels, plane), f32),
        in_specs=[vmem] * 6
        + [pl.BlockSpec(memory_space=pltpu.SMEM), pl.BlockSpec(memory_space=pl.ANY)],
        out_specs=vmem,
        scratch_shapes=[
            pltpu.VMEM((groups_y, *slab_x), f32),
            pltpu.VMEM((groups_y, *slab_x), f32),
            pltpu.VMEM(slab_x, f32),
            pltpu.VMEM((groups_x, *slab_x), f32),
            pltpu.VMEM(slab_k, f32),
            pltpu.VMEM((groups_x, *slab_k), f32),
            pltpu.VMEM(slab_x, f32),
            pltpu.VMEM((groups_y, *slab_x), f32),
            pltpu.VMEM(spectral_weight.shape, f32),
            pltpu.SemaphoreType.DMA((4, max(groups_x, groups_y))),
            pltpu.SemaphoreType.DMA((4, max(groups_x, groups_y))),
            pltpu.SemaphoreType.DMA,
        ],
        compiler_params=pltpu.CompilerParams(
            collective_id=0, has_side_effects=True, vmem_limit_bytes=32 * 1024 * 1024
        ),
    )(cells.reshape(cells_x * channels, plane), *tables, spectral_weight)


def spectral_general(volume, spectral_weight):
    channels, cells_x, cells_y, _ = volume.shape
    total_x = cells_x * lax.axis_size("gx")
    total_y = cells_y * lax.axis_size("gy")
    merged = channels * KZ
    depth_modes = jnp.arange(KZ, dtype=jnp.int32)
    depth_cells = jnp.arange(NZ, dtype=jnp.int32)
    depth_angles = (depth_cells[:, None] * depth_modes[None, :] % NZ).astype(jnp.float32) * (
        2.0 * math.pi / NZ
    )
    depth_forward = jnp.stack([jnp.cos(depth_angles), -jnp.sin(depth_angles)], axis=1)
    along_z = jnp.einsum("cxyz,zqk->xyqck", volume, depth_forward, precision=exact_precision)
    along_z = along_z.reshape(cells_x, cells_y, 2, merged)
    table_x = forward_table(KX, total_x, lax.axis_index("gx") * cells_x, cells_x)
    table_y = forward_table(KY, total_y, lax.axis_index("gy") * cells_y, cells_y)
    inverse_x = jnp.transpose(table_x, (2, 3, 0, 1))
    inverse_y = jnp.transpose(table_y, (2, 3, 0, 1))
    part_x = jnp.einsum("kpxq,xyqm->kypm", table_x, along_z, precision=exact_precision)
    summed_x = lax.psum_scatter(part_x, "gx", scatter_dimension=0, tiled=True)
    partials = jnp.einsum("jpyq,kyqm->kjpm", table_y, summed_x, precision=exact_precision)
    owned_modes = lax.psum_scatter(partials, "gy", scatter_dimension=1, tiled=True)
    mixed_modes = mix_modes(owned_modes, spectral_weight, channels)
    whole_y = lax.all_gather(mixed_modes, "gy", axis=1, tiled=True)
    back_y = jnp.einsum("ypjq,kjqm->kypm", inverse_y, whole_y, precision=exact_precision)
    whole_x = lax.all_gather(back_y, "gx", axis=0, tiled=True)
    back_x = jnp.einsum("xpkq,kyqm->xypm", inverse_x, whole_x, precision=exact_precision)
    weights_z = jnp.where(depth_modes == 0, 1.0, 2.0).astype(jnp.float32) / (total_x * total_y * NZ)
    inverse_angles = jnp.transpose(depth_angles)
    depth_inverse = jnp.stack(
        [
            weights_z[:, None] * jnp.cos(inverse_angles),
            -weights_z[:, None] * jnp.sin(inverse_angles),
        ],
        axis=0,
    )
    fourier = jnp.einsum(
        "xyqck,qkz->cxyz",
        back_x.reshape(cells_x, cells_y, 2, channels, KZ),
        depth_inverse,
        precision=exact_precision,
    )
    return fourier.reshape(channels, cells_x, cells_y * NZ)


def per_device(
    state_field, spectral_weight, conv_fine, conv_coarse, conv_mix, linear_weight, bias_vector
):
    channels, cells_x, plane = state_field.shape
    cells_y = plane // NZ
    volume = state_field.reshape(channels, cells_x, cells_y, NZ)
    padded = extended(volume, (("gx", 1), ("gy", 2)), 1)
    fine_level = jax.nn.gelu(conv_merged(padded, conv_fine, cells_x, cells_y, NZ))
    pooled = fine_level.reshape(channels, cells_x // 2, 2, cells_y // 2, 2, NZ // 2, 2).mean(
        axis=(2, 4, 6)
    )
    coarse_padded = extended(pooled, (("gx", 1), ("gy", 2)), 1)
    coarse = jax.nn.gelu(
        conv_merged(coarse_padded, conv_coarse, cells_x // 2, cells_y // 2, NZ // 2)
    )
    coarse = coarse.reshape(channels, cells_x // 2, 1, cells_y // 2, 1, NZ // 2, 1)
    spread = jnp.broadcast_to(coarse, (channels, cells_x // 2, 2, cells_y // 2, 2, NZ // 2, 2))
    joined = fine_level + spread.reshape(channels, cells_x, cells_y * NZ)
    unet_branch = jnp.einsum("oi,ixw->oxw", conv_mix, joined, precision=exact_precision)
    pointwise = jnp.einsum("oi,ixw->oxw", linear_weight, state_field, precision=exact_precision)
    rows_y = spectral_weight.shape[1]
    if 2 * rows_y * KZ == 128 and 2 * rows_y == 8 and channels % 8 == 0 and plane % 128 == 0:
        cells = jnp.transpose(state_field, (1, 0, 2))
        fourier = spectral(cells, spectral_weight, cells_y)
        fourier = jnp.transpose(fourier.reshape(cells_x, channels, plane), (1, 0, 2))
    else:
        fourier = spectral_general(volume, spectral_weight)
    summed = fourier + unet_branch + pointwise + bias_vector[:, None, None]
    return jax.nn.gelu(summed)


def solution(mesh):
    placed = (P(None, "gx", "gy"), P("gx", "gy", None, None, None), P(), P(), P(), P(), P())
    return jax.shard_map(
        per_device, mesh=mesh, in_specs=placed, out_specs=P(None, "gx", "gy"), check_vma=False
    )
```

profile of v0, /device:TPU:25, one launch (start us, length us, event | category | flops | bytes accessed | tf_op | source)
XLA Modules:
  0.0 125.6 jit_solution(6873606294731008029)
XLA Ops:
  0.0 1.2 reshape.56
  1.3 1.3 %collective-permute-start = (f32[32,1,8,32]{3,2,0,1:T(8,128)S(1)}, f32[32,1,8,32]{3,2,0,1:T(8,128)S(1)}, u32[]{:S(2)}, u32[]{:S(2)}) collective-permute-start(f32[32,1,8,32]{3,2,0,1:T(8,128)S(1)} %copy.54), channel_id=1, source_target_pairs={{0,8},{8,16},{16,24},{1,9},{9,17},{17,25},{2,10},{10,18},{18,26},{... | collective-permute-start | bytes 98312 | tf_op jit(solution)/shard_map/ppermute | solution.py:29
  2.6 4.0 %collective-permute-start.1 = (f32[32,1,8,32]{3,2,0,1:T(8,128)S(1)}, f32[32,1,8,32]{3,2,0,1:T(8,128)S(1)}, u32[]{:S(2)}, u32[]{:S(2)}) collective-permute-start(f32[32,1,8,32]{3,2,0,1:T(8,128)S(1)} %copy.55), channel_id=1, source_target_pairs={{8,0},{16,8},{24,16},{9,1},{17,9},{25,17},{10,2},{18,10},{26,18},{... | collective-permute-start | bytes 98312 | tf_op jit(solution)/shard_map/ppermute | solution.py:31
  6.6 0.9 collective-permute-done
  7.7 0.9 collective-permute-done.1
  8.8 4.8 %collective-permute-start.2 = (f32[32,10,1,32]{3,2,0,1:T(1,128)S(1)}, f32[32,10,1,32]{3,2,0,1:T(1,128)S(1)}, u32[]{:S(2)}, u32[]{:S(2)}) collective-permute-start(f32[32,10,1,32]{3,2,0,1:T(1,128)S(1)} %get-tuple-element.5), channel_id=1, source_target_pairs={{0,1},{1,2},{2,3},{3,4},{4,5},{5,6},{6,7},{8,9},{9,10},{10,11},{11... | collective-permute-start | bytes 122888 | tf_op jit(solution)/shard_map/ppermute | solution.py:29
  13.6 1.9 %collective-permute-start.3 = (f32[32,10,1,32]{3,2,0,1:T(1,128)S(1)}, f32[32,10,1,32]{3,2,0,1:T(1,128)S(1)}, u32[]{:S(2)}, u32[]{:S(2)}) collective-permute-start(f32[32,10,1,32]{3,2,0,1:T(1,128)S(1)} %get-tuple-element.6), channel_id=1, source_target_pairs={{1,0},{2,1},{3,2},{4,3},{5,4},{6,5},{7,6},{9,8},{10,9},{11,10},{12... | collective-permute-start | bytes 122888 | tf_op jit(solution)/shard_map/ppermute | solution.py:31
  15.9 4.4 %collective-permute-done.3 = f32[32,10,1,32]{3,2,0,1:T(1,128)S(1)} collective-permute-done((f32[32,10,1,32]{3,2,0,1:T(1,128)S(1)}, f32[32,10,1,32]{3,2,0,1:T(1,128)S(1)}, u32[]{:S(2)}, u32[]{:S(2)}) %collective-permute-start.3) | collective-permute-done | bytes 40992 | tf_op jit(solution)/shard_map/ppermute | solution.py:31
  20.3 0.6 pad_maximum_fusion
  20.9 0.6 reshape.57
  21.5 1.1 convolution_multiply_fusion.16
  22.6 1.1 convolution_multiply_fusion.14
  23.7 1.1 convolution_multiply_fusion.12
  30.1 0.4 fusion.20
  30.8 0.4 fusion.15
  31.6 0.4 fusion.10
  32.3 0.4 fusion.5
  32.6 0.4 fusion.66
  33.1 0.7 copy-done.8
  34.2 1.4 %reduce_sum.9 = f32[32,4,4,16]{0,3,2,1:T(8,128)} reduce(f32[32,4,2,4,2,16,2]{0,6,5,4,3,2,1:T(2,128)S(1)} %bitcast.336, f32[]{:T(128)} %constant.29.clone.1), dimensions={2,4,6}, to_apply=%region_0.1 | reduce | flops 57344 | bytes 294916 | tf_op jit(solution)/shard_map/reduce_sum | solution.py:378
  35.6 0.9 broadcast_multiply_fusion
  36.5 1.3 %collective-permute-start.4 = (f32[32,1,4,16]{0,3,2,1:T(8,128)S(1)}, f32[32,1,4,16]{0,3,2,1:T(8,128)S(1)}, u32[]{:S(2)}, u32[]{:S(2)}) collective-permute-start(f32[32,1,4,16]{0,3,2,1:T(8,128)S(1)} %get-tuple-element.11), channel_id=1, source_target_pairs={{0,8},{8,16},{16,24},{1,9},{9,17},{17,25},{2,10},{10,18},{18,26},{... | collective-permute-start | bytes 24584 | tf_op jit(solution)/shard_map/ppermute | solution.py:29
  37.8 4.7 %collective-permute-start.5 = (f32[32,1,4,16]{0,3,2,1:T(8,128)S(1)}, f32[32,1,4,16]{0,3,2,1:T(8,128)S(1)}, u32[]{:S(2)}, u32[]{:S(2)}) collective-permute-start(f32[32,1,4,16]{0,3,2,1:T(8,128)S(1)} %get-tuple-element.12), channel_id=1, source_target_pairs={{8,0},{16,8},{24,16},{9,1},{17,9},{25,17},{10,2},{18,10},{26,18},{... | collective-permute-start | bytes 24584 | tf_op jit(solution)/shard_map/ppermute | solution.py:31
  42.6 1.0 collective-permute-done.5
  43.6 2.6 %collective-permute-start.6 = (f32[32,6,1,16]{0,3,2,1:T(8,128)S(1)}, f32[32,6,1,16]{0,3,2,1:T(8,128)S(1)}, u32[]{:S(2)}, u32[]{:S(2)}) collective-permute-start(f32[32,6,1,16]{0,3,2,1:T(8,128)S(1)} %get-tuple-element.9), channel_id=1, source_target_pairs={{0,1},{1,2},{2,3},{3,4},{4,5},{5,6},{6,7},{8,9},{9,10},{10,11},{11... | collective-permute-start | bytes 36872 | tf_op jit(solution)/shard_map/ppermute | solution.py:29
  46.2 2.1 %collective-permute-start.7 = (f32[32,6,1,16]{0,3,2,1:T(8,128)S(1)}, f32[32,6,1,16]{0,3,2,1:T(8,128)S(1)}, u32[]{:S(2)}, u32[]{:S(2)}) collective-permute-start(f32[32,6,1,16]{0,3,2,1:T(8,128)S(1)} %get-tuple-element.10), channel_id=1, source_target_pairs={{1,0},{2,1},{3,2},{4,3},{5,4},{6,5},{7,6},{9,8},{10,9},{11,10},{12... | collective-permute-start | bytes 36872 | tf_op jit(solution)/shard_map/ppermute | solution.py:31
  48.5 2.2 %copy-done.1 = f32[8,4,2,32,512]{4,3,2,1,0:T(8,128)S(1)} copy-done((f32[8,4,2,32,512]{4,3,2,1,0:T(8,128)S(1)}, f32[8,4,2,32,512]{4,3,2,1,0:T(8,128)}, u32[]{:S(2)}) %copy-start.1) | copy-done | bytes 4194328
  50.7 65.5 %shard_map.127 = f32[256,256]{1,0:T(8,128)S(1)} custom-call(f32[256,256]{1,0:T(8,128)S(1)} %bitcast.333, bf16[8,256,128]{2,1,0:T(8,128)(2,1)S(1)} %copy-done.2, bf16[8,256,128]{2,1,0:T(8,128)(2,1)S(1)} %copy-done.3, bf16[8,128,256]{2,1,0:T(8,128)(2,1)S(1)} %copy-done.4, bf16[8,128,256]{2,1,0:T(8,128)(2,1)S(1)} %copy-done.5, f32[64,2,128]{2,1,0:T(2,128)S(1)} %copy-done.6, ...), custom_call_target="tpu_custom_call" | custom-call | tf_op jit(solution)/shard_map/pallas_call | solution.py:298
  122.9 0.5 broadcast_in_dim.5
  124.0 0.4 copy-done.11
  124.4 0.4 fusion.73
  124.8 0.9 copy.50
  (99 shorter events, 14.5 us)
Async XLA Ops:
  0.0 123.7 %copy-start = (f32[32,32]{1,0:T(8,128)S(1)}, f32[32,32]{1,0:T(8,128)}, u32[]{:S(2)}) copy-start(f32[32,32]{1,0:T(8,128)} %param.17) | copy-start | bytes 12292
  1.3 6.3 %collective-permute-start = (f32[32,1,8,32]{3,2,0,1:T(8,128)S(1)}, f32[32,1,8,32]{3,2,0,1:T(8,128)S(1)}, u32[]{:S(2)}, u32[]{:S(2)}) collective-permute-start(f32[32,1,8,32]{3,2,0,1:T(8,128)S(1)} %copy.54), channel_id=1, source_target_pairs={{0,8},{8,16},{16,24},{1,9},{9,17},{17,25},{2,10},{10,18},{18,26},{... | collective-permute-start | bytes 98312 | tf_op jit(solution)/shard_map/ppermute | solution.py:29
  2.6 5.9 %collective-permute-start.1 = (f32[32,1,8,32]{3,2,0,1:T(8,128)S(1)}, f32[32,1,8,32]{3,2,0,1:T(8,128)S(1)}, u32[]{:S(2)}, u32[]{:S(2)}) collective-permute-start(f32[32,1,8,32]{3,2,0,1:T(8,128)S(1)} %copy.55), channel_id=1, source_target_pairs={{8,0},{16,8},{24,16},{9,1},{17,9},{25,17},{10,2},{18,10},{26,18},{... | collective-permute-start | bytes 98312 | tf_op jit(solution)/shard_map/ppermute | solution.py:31
  8.8 7.1 %collective-permute-start.2 = (f32[32,10,1,32]{3,2,0,1:T(1,128)S(1)}, f32[32,10,1,32]{3,2,0,1:T(1,128)S(1)}, u32[]{:S(2)}, u32[]{:S(2)}) collective-permute-start(f32[32,10,1,32]{3,2,0,1:T(1,128)S(1)} %get-tuple-element.5), channel_id=1, source_target_pairs={{0,1},{1,2},{2,3},{3,4},{4,5},{5,6},{6,7},{8,9},{9,10},{10,11},{11... | collective-permute-start | bytes 122888 | tf_op jit(solution)/shard_map/ppermute | solution.py:29
  13.6 6.6 %collective-permute-start.3 = (f32[32,10,1,32]{3,2,0,1:T(1,128)S(1)}, f32[32,10,1,32]{3,2,0,1:T(1,128)S(1)}, u32[]{:S(2)}, u32[]{:S(2)}) collective-permute-start(f32[32,10,1,32]{3,2,0,1:T(1,128)S(1)} %get-tuple-element.6), channel_id=1, source_target_pairs={{1,0},{2,1},{3,2},{4,3},{5,4},{6,5},{7,6},{9,8},{10,9},{11,10},{12... | collective-permute-start | bytes 122888 | tf_op jit(solution)/shard_map/ppermute | solution.py:31
  21.5 3.3 %copy-start.12 = (f32[27,32,32]{2,1,0:T(8,128)S(1)}, f32[27,32,32]{2,1,0:T(8,128)}, u32[]{:S(2)}) copy-start(f32[27,32,32]{2,1,0:T(8,128)} %param.15) | copy-start | bytes 331780
  33.1 0.7 copy-start.8
  33.8 14.5 %copy-start.10 = (f32[32,8,256]{2,1,0:T(8,128)S(1)}, f32[32,8,256]{2,1,0:T(8,128)}, u32[]{:S(2)}) copy-start(f32[32,8,256]{2,1,0:T(8,128)} %param.13) | copy-start | bytes 786436
  34.1 14.3 %copy-start.2 = (bf16[8,256,128]{2,1,0:T(8,128)(2,1)S(1)}, bf16[8,256,128]{2,1,0:T(8,128)(2,1)}, u32[]{:S(2)}) copy-start(bf16[8,256,128]{2,1,0:T(8,128)(2,1)} %constant.66.clone.fwd_high) | copy-start | bytes 1572868
  34.1 14.3 %copy-start.3 = (bf16[8,256,128]{2,1,0:T(8,128)(2,1)S(1)}, bf16[8,256,128]{2,1,0:T(8,128)(2,1)}, u32[]{:S(2)}) copy-start(bf16[8,256,128]{2,1,0:T(8,128)(2,1)} %constant.67.clone.fwd_low) | copy-start | bytes 1572868
  34.1 14.3 %copy-start.4 = (bf16[8,128,256]{2,1,0:T(8,128)(2,1)S(1)}, bf16[8,128,256]{2,1,0:T(8,128)(2,1)}, u32[]{:S(2)}) copy-start(bf16[8,128,256]{2,1,0:T(8,128)(2,1)} %constant.68.clone.inv_high) | copy-start | bytes 1572868
  34.2 14.3 %copy-start.5 = (bf16[8,128,256]{2,1,0:T(8,128)(2,1)S(1)}, bf16[8,128,256]{2,1,0:T(8,128)(2,1)}, u32[]{:S(2)}) copy-start(bf16[8,128,256]{2,1,0:T(8,128)(2,1)} %constant.69.clone.inv_low) | copy-start | bytes 1572868
  34.2 14.3 %copy-start.6 = (f32[64,2,128]{2,1,0:T(2,128)S(1)}, f32[64,2,128]{2,1,0:T(2,128)}, u32[]{:S(2)}) copy-start(f32[64,2,128]{2,1,0:T(2,128)} %constant.70.clone.rotation) | copy-start | bytes 196612
  34.2 14.3 %copy-start.7 = (f32[2048]{0:T(1024)S(1)}, f32[2048]{0:T(1024)}, u32[]{:S(2)}) copy-start(f32[2048]{0:T(1024)} %constant.71.clone.table_x) | copy-start | bytes 24580
  36.5 6.0 %collective-permute-start.4 = (f32[32,1,4,16]{0,3,2,1:T(8,128)S(1)}, f32[32,1,4,16]{0,3,2,1:T(8,128)S(1)}, u32[]{:S(2)}, u32[]{:S(2)}) collective-permute-start(f32[32,1,4,16]{0,3,2,1:T(8,128)S(1)} %get-tuple-element.11), channel_id=1, source_target_pairs={{0,8},{8,16},{16,24},{1,9},{9,17},{17,25},{2,10},{10,18},{18,26},{... | collective-permute-start | bytes 24584 | tf_op jit(solution)/shard_map/ppermute | solution.py:29
  37.8 5.7 %collective-permute-start.5 = (f32[32,1,4,16]{0,3,2,1:T(8,128)S(1)}, f32[32,1,4,16]{0,3,2,1:T(8,128)S(1)}, u32[]{:S(2)}, u32[]{:S(2)}) collective-permute-start(f32[32,1,4,16]{0,3,2,1:T(8,128)S(1)} %get-tuple-element.12), channel_id=1, source_target_pairs={{8,0},{16,8},{24,16},{9,1},{17,9},{25,17},{10,2},{18,10},{26,18},{... | collective-permute-start | bytes 24584 | tf_op jit(solution)/shard_map/ppermute | solution.py:31
  43.6 72.6 %collective-permute-start.6 = (f32[32,6,1,16]{0,3,2,1:T(8,128)S(1)}, f32[32,6,1,16]{0,3,2,1:T(8,128)S(1)}, u32[]{:S(2)}, u32[]{:S(2)}) collective-permute-start(f32[32,6,1,16]{0,3,2,1:T(8,128)S(1)} %get-tuple-element.9), channel_id=1, source_target_pairs={{0,1},{1,2},{2,3},{3,4},{4,5},{5,6},{6,7},{8,9},{9,10},{10,11},{11... | collective-permute-start | bytes 36872 | tf_op jit(solution)/shard_map/ppermute | solution.py:29
  46.2 70.0 %collective-permute-start.7 = (f32[32,6,1,16]{0,3,2,1:T(8,128)S(1)}, f32[32,6,1,16]{0,3,2,1:T(8,128)S(1)}, u32[]{:S(2)}, u32[]{:S(2)}) collective-permute-start(f32[32,6,1,16]{0,3,2,1:T(8,128)S(1)} %get-tuple-element.10), channel_id=1, source_target_pairs={{1,0},{2,1},{3,2},{4,3},{5,4},{6,5},{7,6},{9,8},{10,9},{11,10},{12... | collective-permute-start | bytes 36872 | tf_op jit(solution)/shard_map/ppermute | solution.py:31
  48.5 2.2 %copy-start.1 = (f32[8,4,2,32,512]{4,3,2,1,0:T(8,128)S(1)}, f32[8,4,2,32,512]{4,3,2,1,0:T(8,128)}, u32[]{:S(2)}) copy-start(f32[8,4,2,32,512]{4,3,2,1,0:T(8,128)} %weight_hbm.1) | copy-start | bytes 12582916
  50.7 65.7 %copy-start.13 = (f32[27,32,32]{2,1,0:T(8,128)S(1)}, f32[27,32,32]{2,1,0:T(8,128)}, u32[]{:S(2)}) copy-start(f32[27,32,32]{2,1,0:T(8,128)} %param.16) | copy-start | bytes 331780
  122.8 1.0 copy-start.9
  123.4 1.0 copy-start.11
  123.4 1.0 copy-start.14
  123.4 1.0 copy-start.15
where the time goes:
time: 126 us
  Pallas kernels  65.5 us (52%)
  starting transfers between devices  22.7 us (18%)
  matrix products  18.2 us (14%)
  local copies, waits for them, and re-layouts  7.85 us (6%)
  waiting for transfers between devices  7.51 us (6%)
  other arithmetic  2.98 us (2%)
    pallas_call x1, Pallas kernels, spectral(): pl.pallas_call(functools.partial(spectral_kernel, groups_x, groups_y, cel...  65.5 us
    dot_general x54, matrix products, conv_merged(): jnp.einsum('oi,ixw->oxw', weight[offset], window, precision=exact_precision)  17.6 us
    ppermute x4, starting transfers between devices, extended(): lax.ppermute(head, axis, [((i + 1) % count, i) for i in range(ends)])  12.7 us
    ppermute x4, starting transfers between devices, extended(): lax.ppermute(tail, axis, [(i, (i + 1) % count) for i in range(ends)])  10 us
    ppermute x4, waiting for transfers between devices, extended(): lax.ppermute(head, axis, [((i + 1) % count, i) for i in range(ends)])  6.26 us
    unnamed x36, local copies, waits for them, and re-layouts  3.43 us
  transfers between devices with their start and end apart: 8, of which 5 were waited for; matrix products, arithmetic and copies ran while one was open for 0% of the time, Pallas kernels for 52%

commit v1 on v0

--- a/solution.py
+++ b/solution.py
@@ -149,9 +149,13 @@
 def spectral_kernel(
     groups_x, groups_y, cells_x, rows_x, rows_y, channels,
     cells_ref, fwd_high, fwd_low, inv_high, inv_low, rotation, table_x, weight_hbm,
+    fine_ref, coarse_ref, point_ref, bias_ref, pool_ref, spread_ref,
     out_ref,
     parts, parts_in, line, line_in, mixed, mixed_in, back, back_in, weight,
     send_sem, recv_sem, weight_sem,
+    edges, edges_in, planes_in, corners_in, padded, stack_high, stack_low, sums, fine,
+    pooled, rim, rim_in, pooled_in, rim_corners_in, coarse_padded, base,
+    halo_send, halo_recv,
 ):
     mx, my = lax.axis_index("gx"), lax.axis_index("gy")
     lanes = 2 * rows_y * KZ
@@ -168,7 +172,54 @@
         pl.semaphore_signal(
             barrier, inc=1, device_id=(lax.rem(mx + step, groups_x), my), device_id_type=MESH
         )
-    pl.semaphore_wait(barrier, groups_x + groups_y - 2)
+    up_x, down_x = lax.rem(mx + 1, groups_x), lax.rem(mx + groups_x - 1, groups_x)
+    up_y, down_y = lax.rem(my + 1, groups_y), lax.rem(my + groups_y - 1, groups_y)
+    sides_x, sides_y = (down_x, up_x), (down_y, up_y)
+    for to_x in sides_x:
+        for to_y in sides_y:
+            pl.semaphore_signal(barrier, inc=1, device_id=(to_x, to_y), device_id_type=MESH)
+    pl.semaphore_wait(barrier, groups_x + groups_y + 2)
+
+    def halo(phase, index, source, target, device):
+        copy = pltpu.make_async_remote_copy(
+            src_ref=source, dst_ref=target,
+            send_sem=halo_send.at[phase, index], recv_sem=halo_recv.at[phase, index],
+            device_id=device, device_id_type=MESH,
+        )
+        copy.start()
+        return copy
+
+    def rows_of(plane):
+        return pl.ds(plane * channels, channels)
+
+    lane_full = lax.broadcasted_iota(jnp.int32, (channels, 128), 1)
+    plane_lanes = cells_ref.shape[1]
+    per_tile = 128 // NZ
+    last_tile = cells_x // per_tile - 1
+    for tile in range(cells_x // per_tile):
+        first = jnp.zeros((channels, 128), jnp.float32)
+        last = jnp.zeros((channels, 128), jnp.float32)
+        for slot in range(per_tile):
+            rows = rows_of(tile * per_tile + slot)
+            here = lane_full // NZ == slot
+            head = cells_ref[rows, 0:128]
+            tail = cells_ref[rows, plane_lanes - 128 : plane_lanes]
+            first = jnp.where(here, pltpu.roll(head, slot * NZ, 1), first)
+            last = jnp.where(here, pltpu.roll(tail, (slot * NZ + NZ) % 128, 1), last)
+        edges[0, tile] = first
+        edges[1, tile] = last
+    halos = []
+    for side in range(2):
+        edge_plane = cells_ref.at[rows_of(side * (cells_x - 1)), :]
+        halos.append(halo(0, side, edge_plane, planes_in.at[1 - side], (sides_x[side], my)))
+        halos.append(halo(0, 2 + side, edges.at[side], edges_in.at[1 - side], (mx, sides_y[side])))
+        for other in range(2):
+            halos.append(
+                halo(
+                    0, 4 + 2 * side + other, edges.at[other, side * last_tile],
+                    corners_in.at[1 - side, 1 - other], (sides_x[side], sides_y[other]),
+                )
+            )
 
     def send(phase, step, source, target, device):
         copy = pltpu.make_async_remote_copy(
@@ -192,6 +243,86 @@
         parts[step] = part
         if step:
             copies.append(send(0, step, parts.at[step], parts_in.at[step], (mx, peer)))
+    f32 = jnp.float32
+    at_x = ((mx > 0).astype(f32), (mx < groups_x - 1).astype(f32))
+    at_y = ((my > 0).astype(f32), (my < groups_y - 1).astype(f32))
+    for copy in halos:
+        copy.wait()
+
+    def fill(plane, main, left, right, left_slot, right_slot, scale):
+        padded[plane, :, 0:128] = (
+            pltpu.roll(left, (128 - NZ - left_slot * NZ) % 128, 1) * (at_y[0] * scale)
+        )
+        padded[plane, :, 128 : 128 + plane_lanes] = main * scale
+        padded[plane, :, 128 + plane_lanes : 256 + plane_lanes] = (
+            pltpu.roll(right, (128 - right_slot * NZ) % 128, 1) * (at_y[1] * scale)
+        )
+
+    for x in range(cells_x):
+        tile, slot = x // per_tile, x % per_tile
+        fill(x + 1, cells_ref[rows_of(x), :], edges_in[0, tile], edges_in[1, tile], slot, slot, 1.0)
+    end = per_tile - 1
+    fill(0, planes_in[0], corners_in[0, 0], corners_in[0, 1], end, end, at_x[0])
+    fill(cells_x + 1, planes_in[1], corners_in[1, 0], corners_in[1, 1], 0, 0, at_x[1])
+
+    def convolve(source, kernel, count, width, start, depth):
+        kernel_high, kernel_low = split_pair(kernel)
+        total_lanes = source.shape[2]
+        depths = lax.broadcasted_iota(jnp.int32, (channels, width), 1) % depth
+        for slot in range(count + 4):
+            sums[slot, :, 0:width] = jnp.zeros((channels, width), f32)
+
+        def one_plane(plane, carry):
+            values = source[plane]
+            for tap in range(9):
+                shift_y, shift_z = tap // 3 - 1, tap % 3 - 1
+                moved = pltpu.roll(values, (-shift_y * depth - shift_z) % total_lanes, 1)
+                moved = moved[:, start : start + width]
+                if shift_z == -1:
+                    moved = jnp.where(depths > 0, moved, 0.0)
+                elif shift_z == 1:
+                    moved = jnp.where(depths < depth - 1, moved, 0.0)
+                high, low = split_pair(moved)
+                stack_high[tap * channels : (tap + 1) * channels, 0:width] = high
+                stack_low[tap * channels : (tap + 1) * channels, 0:width] = low
+            high, low = stack_high[:, 0:width], stack_low[:, 0:width]
+            term = dot(kernel_high, high) + dot(kernel_high, low) + dot(kernel_low, high)
+            for shift_x in range(3):
+                piece = term[shift_x * channels : (shift_x + 1) * channels]
+                slot = plane - shift_x + 2
+                sums[slot, :, 0:width] = sums[slot, :, 0:width] + piece
+            return carry
+
+        lax.fori_loop(0, count + 2, one_plane, 0)
+
+    convolve(padded, fine_ref[...], cells_x, plane_lanes, 128, NZ)
+    pairs = cells_x // 2
+    short = NZ // 2
+    for x in range(cells_x):
+        fine[x] = jax.nn.gelu(sums[x + 2])
+    for pair in range(pairs):
+        high, low = split_pair(fine[2 * pair] + fine[2 * pair + 1])
+        pooled[pair] = dot(high, pool_ref[...]) + dot(low, pool_ref[...])
+    packed = jnp.zeros((channels, 128), f32)
+    for pair in range(pairs):
+        values = pooled[pair]
+        slot = lane_full // short
+        packed = jnp.where(slot == pair, pltpu.roll(values, (pair * short - short) % 128, 1), packed)
+        packed = jnp.where(slot == pairs + pair, pltpu.roll(values, pair * short, 1), packed)
+    rim[...] = packed
+    rims = []
+    for side in range(2):
+        rims.append(
+            halo(1, side, pooled.at[side * (pairs - 1)], pooled_in.at[1 - side], (sides_x[side], my))
+        )
+        rims.append(halo(1, 2 + side, rim, rim_in.at[1 - side], (mx, sides_y[side])))
+        for other in range(2):
+            rims.append(
+                halo(
+                    1, 4 + 2 * side + other, rim, rim_corners_in.at[1 - side, 1 - other],
+                    (sides_x[side], sides_y[other]),
+                )
+            )
     total = parts[0]
     for step, copy in enumerate(copies, 1):
         copy.wait()
@@ -201,6 +332,31 @@
         send(1, step, line, line_in.at[step], (lax.rem(mx + step, groups_x), my))
         for step in range(1, groups_x)
     ]
+    for copy in rims:
+        copy.wait()
+    inner = short * (pairs + 1)
+
+    def fill_coarse(plane, main, left, right, slot, scale):
+        before = pltpu.roll(left, (128 - (pairs + slot) * short) % 128, 1) * at_y[0]
+        after = pltpu.roll(right, (inner - slot * short) % 128, 1) * at_y[1]
+        values = jnp.where(lane_full < short, before, main)
+        values = jnp.where(lane_full // short == pairs + 1, after, values)
+        coarse_padded[plane] = values * scale
+
+    for pair in range(pairs):
+        fill_coarse(pair + 1, pooled[pair], rim_in[0], rim_in[1], pair, 1.0)
+    fill_coarse(0, pooled_in[0], rim_corners_in[0, 0], rim_corners_in[0, 1], pairs - 1, at_x[0])
+    fill_coarse(pairs + 1, pooled_in[1], rim_corners_in[1, 0], rim_corners_in[1, 1], 0, at_x[1])
+    convolve(coarse_padded, coarse_ref[...], pairs, 128, 0, short)
+    point_high, point_low = split_pair(point_ref[...])
+    for pair in range(pairs):
+        high, low = split_pair(jax.nn.gelu(sums[pair + 2, :, 0:128]))
+        raised = dot(high, spread_ref[...]) + dot(low, spread_ref[...])
+        for x in (2 * pair, 2 * pair + 1):
+            joined = jnp.concatenate([fine[x] + raised, cells_ref[rows_of(x), :]], axis=0)
+            high, low = split_pair(joined)
+            value = dot(point_high, high) + dot(point_high, low) + dot(point_low, high)
+            base[rows_of(x), :] = value + bias_ref[...]
     for copy in copies:
         copy.wait()
     load_weight.wait()
@@ -283,10 +439,26 @@
         values = values * turn[0:1] - pltpu.roll(values, half, 1) * turn[1:2]
         term = dot_split(values, inv_high[peer], inv_low[peer])
         result = term if result is None else result + term
-    out_ref[...] = result
-
-
-def spectral(cells, spectral_weight, cells_y):
+    out_ref[...] = jax.nn.gelu(result + base[...])
+
+
+def stacked(weight):
+    taps, outs, ins = weight.shape
+    return weight.reshape(3, 9, outs, ins).transpose(0, 2, 1, 3).reshape(3 * outs, 9 * ins)
+
+
+def pooling(cells_y):
+    cells = np.arange(cells_y * NZ)
+    short = NZ // 2
+    place = short + cells // NZ // 2 * short + cells % NZ // 2
+    hit = place[:, None] == np.arange(128)[None, :]
+    pool = jnp.asarray((hit * 0.125).astype(jnp.bfloat16))
+    return pool, jnp.asarray(hit.T.astype(np.float32).astype(jnp.bfloat16))
+
+
+def layer(
+    cells, spectral_weight, conv_fine, conv_coarse, conv_mix, linear_weight, bias_vector, cells_y
+):
     cells_x, channels, plane = cells.shape
     rows_x, rows_y = spectral_weight.shape[:2]
     groups_x, groups_y = lax.axis_size("gx"), lax.axis_size("gy")
@@ -301,7 +473,8 @@
         ),
         out_shape=jax.ShapeDtypeStruct((cells_x * channels, plane), f32),
         in_specs=[vmem] * 6
-        + [pl.BlockSpec(memory_space=pltpu.SMEM), pl.BlockSpec(memory_space=pl.ANY)],
+        + [pl.BlockSpec(memory_space=pltpu.SMEM), pl.BlockSpec(memory_space=pl.ANY)]
+        + [vmem] * 6,
         out_specs=vmem,
         scratch_shapes=[
             pltpu.VMEM((groups_y, *slab_x), f32),
@@ -316,11 +489,34 @@
             pltpu.SemaphoreType.DMA((4, max(groups_x, groups_y))),
             pltpu.SemaphoreType.DMA((4, max(groups_x, groups_y))),
             pltpu.SemaphoreType.DMA,
+            pltpu.VMEM((2, cells_x * NZ // 128, channels, 128), f32),
+            pltpu.VMEM((2, cells_x * NZ // 128, channels, 128), f32),
+            pltpu.VMEM((2, channels, plane), f32),
+            pltpu.VMEM((2, 2, channels, 128), f32),
+            pltpu.VMEM((cells_x + 2, channels, plane + 256), f32),
+            pltpu.VMEM((9 * channels, plane), jnp.bfloat16),
+            pltpu.VMEM((9 * channels, plane), jnp.bfloat16),
+            pltpu.VMEM((cells_x + 4, channels, plane), f32),
+            pltpu.VMEM((cells_x, channels, plane), f32),
+            pltpu.VMEM((cells_x // 2, channels, 128), f32),
+            pltpu.VMEM((channels, 128), f32),
+            pltpu.VMEM((2, channels, 128), f32),
+            pltpu.VMEM((2, channels, 128), f32),
+            pltpu.VMEM((2, 2, channels, 128), f32),
+            pltpu.VMEM((cells_x // 2 + 2, channels, 128), f32),
+            pltpu.VMEM((cells_x * channels, plane), f32),
+            pltpu.SemaphoreType.DMA((2, 8)),
+            pltpu.SemaphoreType.DMA((2, 8)),
         ],
         compiler_params=pltpu.CompilerParams(
             collective_id=0, has_side_effects=True, vmem_limit_bytes=32 * 1024 * 1024
         ),
-    )(cells.reshape(cells_x * channels, plane), *tables, spectral_weight)
+    )(
+        cells.reshape(cells_x * channels, plane), *tables, spectral_weight,
+        stacked(conv_fine), stacked(conv_coarse),
+        jnp.concatenate([conv_mix, linear_weight], axis=1), bias_vector[:, None],
+        *pooling(cells_y),
+    )
 
 
 def spectral_general(volume, spectral_weight):
@@ -372,6 +568,22 @@
 ):
     channels, cells_x, plane = state_field.shape
     cells_y = plane // NZ
+    rows_y = spectral_weight.shape[1]
+    if (
+        2 * rows_y * KZ == 128
+        and 2 * rows_y == 8
+        and channels * KZ % 128 == 0
+        and plane % 128 == 0
+        and cells_x % (128 // NZ) == 0
+        and cells_x * NZ // 2 == 128
+        and cells_x == cells_y
+        and min(lax.axis_size("gx"), lax.axis_size("gy")) > 1
+    ):
+        out = layer(
+            jnp.transpose(state_field, (1, 0, 2)), spectral_weight, conv_fine, conv_coarse,
+            conv_mix, linear_weight, bias_vector, cells_y,
+        )
+        return jnp.transpose(out.reshape(cells_x, channels, plane), (1, 0, 2))
     volume = state_field.reshape(channels, cells_x, cells_y, NZ)
     padded = extended(volume, (("gx", 1), ("gy", 2)), 1)
     fine_level = jax.nn.gelu(conv_merged(padded, conv_fine, cells_x, cells_y, NZ))
@@ -387,13 +599,7 @@
     joined = fine_level + spread.reshape(channels, cells_x, cells_y * NZ)
     unet_branch = jnp.einsum("oi,ixw->oxw", conv_mix, joined, precision=exact_precision)
     pointwise = jnp.einsum("oi,ixw->oxw", linear_weight, state_field, precision=exact_precision)
-    rows_y = spectral_weight.shape[1]
-    if 2 * rows_y * KZ == 128 and 2 * rows_y == 8 and channels % 8 == 0 and plane % 128 == 0:
-        cells = jnp.transpose(state_field, (1, 0, 2))
-        fourier = spectral(cells, spectral_weight, cells_y)
-        fourier = jnp.transpose(fourier.reshape(cells_x, channels, plane), (1, 0, 2))
-    else:
-        fourier = spectral_general(volume, spectral_weight)
+    fourier = spectral_general(volume, spectral_weight)
     summed = fourier + unet_branch + pointwise + bias_vector[:, None, None]
     return jax.nn.gelu(summed)
 

time: 126 us -> 71.7 us (0.57)
  starting transfers between devices: 22.7 us -> 0 us
  matrix products: 18.2 us -> 0 us
  waiting for transfers between devices: 7.51 us -> 0 us
  other arithmetic: 2.98 us -> 0.07 us
    ppermute x8 -> x0, starting transfers between devices: 22.7 us -> none  [the longest x4 12.7 us: extended(): lax.ppermute(head, axis, [((i + 1) % count, i) for i in range(ends)])]
    dot_general x56 -> x0, matrix products: 18.2 us -> none  [the longest x54 17.6 us: conv_merged(): jnp.einsum('oi,ixw->oxw', weight[offset], window, precision=exact_precision)]
    ppermute x8 -> x0, waiting for transfers between devices: 7.51 us -> none  [the longest x4 6.26 us: extended(): lax.ppermute(head, axis, [((i + 1) % count, i) for i in range(ends)])]
    reshape x4 -> x7, local copies, waits for them, and re-layouts: 2.26 us -> 4.27 us  [the longest x6 3.41 us: stacked(): weight.reshape(3, 9, outs, ins).transpose(0, 2, 1, 3)]
    reduce_sum x1 -> x0, other arithmetic: 1.41 us -> none  [per_device(): fine_level.reshape(channels, cells_x // 2, 2, cells_y // 2, 2, NZ // 2, 2)]
    mul x3 -> x0, local copies, waits for them, and re-layouts: 1.28 us -> none  [the longest x1 0.86 us: per_device(): return jax.nn.gelu(summed)]
    unnamed x36 -> x26, local copies, waits for them, and re-layouts: 3.43 us -> 2.25 us
  transfers between devices with their start and end apart: 8 -> 0, of which waited for: 5 -> 0; matrix products, arithmetic and copies ran while one was open for 0% -> 0% of each run, Pallas kernels for 52% -> 0%
where the time goes in v1:
time: 71.7 us; the launch traced here: 71.5 us
  Pallas kernels  64.5 us (90%)
  local copies, waits for them, and re-layouts  6.69 us (9%)
    pallas_call x1, Pallas kernels, layer(): pl.pallas_call(functools.partial(spectral_kernel, groups_x, groups_y, cel...  64.5 us
    reshape x6, local copies, waits for them, and re-layouts, stacked(): weight.reshape(3, 9, outs, ins).transpose(0, 2, 1, 3)  3.41 us
    unnamed x26, local copies, waits for them, and re-layouts  2.25 us

profile of v1, /device:TPU:25, one launch (start us, length us, event | category | flops | bytes accessed | tf_op | source)
XLA Modules:
  0.0 71.5 jit_solution(16741113556892273185)
XLA Ops:
  0.0 0.0 copy-start.4
  0.0 0.0 copy-start.5
  0.0 0.0 copy-start.8
  0.0 0.0 copy-start.6
  0.1 0.0 copy-start.7
  0.1 0.0 copy-start.9
  0.1 0.0 copy-start.12
  0.1 0.0 copy-start.11
  0.1 0.0 copy-start.10
  0.1 1.4 %copy.22 = f32[3,9,32,32]{2,0,3,1:T(4,128)S(1)} copy(f32[3,9,32,32]{3,2,1,0:T(8,128)} %bitcast.19) | data formatting | bytes 221184 | tf_op jit(solution)/shard_map/reshape | solution.py:447
  1.5 0.2 reshape.20
  1.8 0.1 copy.24.fine_ref
  1.9 1.3 %copy.23 = f32[3,9,32,32]{2,0,3,1:T(4,128)S(1)} copy(f32[3,9,32,32]{3,2,1,0:T(8,128)} %bitcast.20) | data formatting | bytes 221184 | tf_op jit(solution)/shard_map/reshape | solution.py:447
  3.2 0.2 reshape.22
  3.4 0.1 copy.25.coarse_ref
  3.5 0.0 copy-done.9
  3.6 0.1 copy.21
  3.6 0.0 copy-done.12
  3.7 0.1 copy.26.bias_ref
  3.7 0.0 copy-done.11
  3.7 0.0 copy-done.10
  3.7 0.1 pad_maximum_fusion.point_ref
  3.8 0.0 copy-done.1
  3.8 0.0 copy-done.4
  3.8 0.0 copy-done.5
  3.9 0.0 copy-done.8
  3.9 0.0 copy-done.6
  3.9 0.0 copy-done.7
  3.9 0.0 copy-start
  3.9 2.2 %copy-done = f32[8,4,2,32,512]{4,3,2,1,0:T(8,128)S(1)} copy-done((f32[8,4,2,32,512]{4,3,2,1,0:T(8,128)S(1)}, f32[8,4,2,32,512]{4,3,2,1,0:T(8,128)}, u32[]{:S(2)}) %copy-start) | copy-done | bytes 4194328
  6.1 64.5 %shard_map.145 = f32[256,256]{1,0:T(8,128)S(1)} custom-call(f32[256,256]{1,0:T(8,128)S(1)} %bitcast.16, bf16[8,256,128]{2,1,0:T(8,128)(2,1)S(1)} %copy-done.1, bf16[8,256,128]{2,1,0:T(8,128)(2,1)S(1)} %copy-done.2, bf16[8,128,256]{2,1,0:T(8,128)(2,1)S(1)} %copy-done.3, bf16[8,128,256]{2,1,0:T(8,128)(2,1)S(1)} %copy-done.4, f32[64,2,128]{2,1,0:T(2,128)S(1)} %copy-done.5, ...), custom_call_target="tpu_custom_call" | custom-call | tf_op jit(solution)/shard_map/pallas_call | solution.py:470
  70.6 0.9 %copy.29 = f32[8,32,256]{2,0,1:T(8,128)} copy(f32[8,32,256]{2,1,0:T(8,128)S(1)} %bitcast.15) | data formatting | bytes 524288 | tf_op jit(solution)/shard_map/reshape | solution.py:586
  (5 shorter events, 0.0 us)
Async XLA Ops:
  0.0 3.8 %copy-start.1 = (bf16[8,256,128]{2,1,0:T(8,128)(2,1)S(1)}, bf16[8,256,128]{2,1,0:T(8,128)(2,1)}, u32[]{:S(2)}) copy-start(bf16[8,256,128]{2,1,0:T(8,128)(2,1)} %constant.16.clone.fwd_high) | copy-start | bytes 1572868
  0.0 3.8 %copy-start.2 = (bf16[8,256,128]{2,1,0:T(8,128)(2,1)S(1)}, bf16[8,256,128]{2,1,0:T(8,128)(2,1)}, u32[]{:S(2)}) copy-start(bf16[8,256,128]{2,1,0:T(8,128)(2,1)} %constant.17.clone.fwd_low) | copy-start | bytes 1572868
  0.0 3.8 %copy-start.3 = (bf16[8,128,256]{2,1,0:T(8,128)(2,1)S(1)}, bf16[8,128,256]{2,1,0:T(8,128)(2,1)}, u32[]{:S(2)}) copy-start(bf16[8,128,256]{2,1,0:T(8,128)(2,1)} %constant.18.clone.inv_high) | copy-start | bytes 1572868
  0.0 3.8 %copy-start.4 = (bf16[8,128,256]{2,1,0:T(8,128)(2,1)S(1)}, bf16[8,128,256]{2,1,0:T(8,128)(2,1)}, u32[]{:S(2)}) copy-start(bf16[8,128,256]{2,1,0:T(8,128)(2,1)} %constant.19.clone.inv_low) | copy-start | bytes 1572868
  0.0 3.8 %copy-start.5 = (f32[64,2,128]{2,1,0:T(2,128)S(1)}, f32[64,2,128]{2,1,0:T(2,128)}, u32[]{:S(2)}) copy-start(f32[64,2,128]{2,1,0:T(2,128)} %constant.20.clone.rotation) | copy-start | bytes 196612
  0.0 3.8 %copy-start.8 = (f32[2048]{0:T(1024)S(1)}, f32[2048]{0:T(1024)}, u32[]{:S(2)}) copy-start(f32[2048]{0:T(1024)} %constant.21.clone.table_x) | copy-start | bytes 24580
  0.0 3.8 %copy-start.6 = (bf16[256,128]{1,0:T(8,128)(2,1)S(1)}, bf16[256,128]{1,0:T(8,128)(2,1)}, u32[]{:S(2)}) copy-start(bf16[256,128]{1,0:T(8,128)(2,1)} %constant.22.clone.pool_ref) | copy-start | bytes 196612
  0.1 3.8 %copy-start.7 = (bf16[128,256]{1,0:T(8,128)(2,1)S(1)}, bf16[128,256]{1,0:T(8,128)(2,1)}, u32[]{:S(2)}) copy-start(bf16[128,256]{1,0:T(8,128)(2,1)} %constant.23.clone.spread_ref) | copy-start | bytes 196612
  0.1 3.5 %copy-start.9 = (f32[32,8,256]{2,1,0:T(8,128)S(1)}, f32[32,8,256]{2,1,0:T(8,128)}, u32[]{:S(2)}) copy-start(f32[32,8,256]{2,1,0:T(8,128)} %param.15) | copy-start | bytes 786436
  0.1 3.6 %copy-start.12 = (f32[32]{0:T(128)S(1)}, f32[32]{0:T(128)}, u32[]{:S(2)}) copy-start(f32[32]{0:T(128)} %param.21) | copy-start | bytes 388
  0.1 3.7 %copy-start.11 = (f32[32,32]{1,0:T(8,128)S(1)}, f32[32,32]{1,0:T(8,128)}, u32[]{:S(2)}) copy-start(f32[32,32]{1,0:T(8,128)} %param.19) | copy-start | bytes 12292
  0.1 3.6 %copy-start.10 = (f32[32,32]{1,0:T(8,128)S(1)}, f32[32,32]{1,0:T(8,128)}, u32[]{:S(2)}) copy-start(f32[32,32]{1,0:T(8,128)} %param.20) | copy-start | bytes 12292
  3.9 2.2 %copy-start = (f32[8,4,2,32,512]{4,3,2,1,0:T(8,128)S(1)}, f32[8,4,2,32,512]{4,3,2,1,0:T(8,128)}, u32[]{:S(2)}) copy-start(f32[8,4,2,32,512]{4,3,2,1,0:T(8,128)} %weight_hbm.1) | copy-start | bytes 12582916

commit v2 on v1

--- a/solution.py
+++ b/solution.py
@@ -151,8 +151,8 @@
     cells_ref, fwd_high, fwd_low, inv_high, inv_low, rotation, table_x, weight_hbm,
     fine_ref, coarse_ref, point_ref, bias_ref, pool_ref, spread_ref,
     out_ref,
-    parts, parts_in, line, line_in, mixed, mixed_in, back, back_in, weight,
-    send_sem, recv_sem, weight_sem,
+    field_in, parts, lines, lines_in, mixed, mixed_in, back, back_in, ready, ready_in, weight,
+    send_sem, recv_sem, relay_send, relay_recv, weight_sem,
     edges, edges_in, planes_in, corners_in, padded, stack_high, stack_low, sums, fine,
     pooled, rim, rim_in, pooled_in, rim_corners_in, coarse_padded, base,
     halo_send, halo_recv,
@@ -192,6 +192,24 @@
     def rows_of(plane):
         return pl.ds(plane * channels, channels)
 
+    def send(phase, step, source, target, device):
+        copy = pltpu.make_async_remote_copy(
+            src_ref=source, dst_ref=target,
+            send_sem=send_sem.at[phase, step], recv_sem=recv_sem.at[phase, step],
+            device_id=device, device_id_type=MESH,
+        )
+        copy.start()
+        return copy
+
+    def aligned(row):
+        return pl.ds(pl.multiple_of(row * channels, channels), channels)
+
+    fields = []
+    for step in range(1, groups_y):
+        peer = lax.rem(my + step, groups_y)
+        fields.append(
+            send(0, step, cells_ref.at[aligned(peer), :], field_in.at[step], (mx, peer))
+        )
     lane_full = lax.broadcasted_iota(jnp.int32, (channels, 128), 1)
     plane_lanes = cells_ref.shape[1]
     per_tile = 128 // NZ
@@ -221,28 +239,43 @@
                 )
             )
 
-    def send(phase, step, source, target, device):
-        copy = pltpu.make_async_remote_copy(
-            src_ref=source, dst_ref=target,
-            send_sem=send_sem.at[phase, step], recv_sem=recv_sem.at[phase, step],
-            device_id=device, device_id_type=MESH,
-        )
-        copy.start()
-        return copy
-
     half = lanes // 2
-    left_high, left_low = split_pair(cells_ref[...])
     dot = functools.partial(jnp.dot, preferred_element_type=jnp.float32)
-    copies = []
+    for copy in fields:
+        copy.wait()
+    sources = [lax.rem(my - step + groups_y, groups_y) for step in range(groups_y)]
+    stack = [cells_ref[aligned(my), :]] + [field_in[step] for step in range(1, groups_y)]
+    left_high, left_low = split_pair(jnp.concatenate(stack, axis=0))
+    copies = [None] * groups_y
     for step in list(range(1, groups_y)) + [0]:
         peer = lax.rem(my + step, groups_y)
         high, low = fwd_high[peer], fwd_low[peer]
         part = dot(left_high, high) + dot(left_high, low) + dot(left_low, high)
-        turn = rotation[my * groups_y + peer]
-        part = part * turn[0:1] + pltpu.roll(part, half, 1) * turn[1:2]
-        parts[step] = part
+        first = jnp.zeros((channels, lanes), jnp.float32)
+        second = jnp.zeros((channels, lanes), jnp.float32)
+        for place, source in enumerate(sources):
+            turn = rotation[source * groups_y + peer]
+            piece = part[place * channels : (place + 1) * channels]
+            first = first + piece * turn[0:1]
+            second = second + piece * turn[1:2]
+        slab = first - pltpu.roll(second, half, 1)
         if step:
-            copies.append(send(0, step, parts.at[step], parts_in.at[step], (mx, peer)))
+            parts[step] = slab
+            copies[step] = send(1, step, parts.at[step], lines.at[step], (mx, peer))
+        else:
+            lines[0] = slab
+    relays = []
+    for step in range(groups_y):
+        if step:
+            copies[step].wait()
+        for hop in range(1, groups_x):
+            relay = pltpu.make_async_remote_copy(
+                src_ref=lines.at[step], dst_ref=lines_in.at[hop, step],
+                send_sem=relay_send.at[hop, step], recv_sem=relay_recv.at[hop, step],
+                device_id=(lax.rem(mx + hop, groups_x), my), device_id_type=MESH,
+            )
+            relay.start()
+            relays.append(relay)
     f32 = jnp.float32
     at_x = ((mx > 0).astype(f32), (mx < groups_x - 1).astype(f32))
     at_y = ((my > 0).astype(f32), (my < groups_y - 1).astype(f32))
@@ -323,41 +356,7 @@
                     (sides_x[side], sides_y[other]),
                 )
             )
-    total = parts[0]
-    for step, copy in enumerate(copies, 1):
-        copy.wait()
-        total = total + parts_in[step]
-    line[...] = total
-    copies = [
-        send(1, step, line, line_in.at[step], (lax.rem(mx + step, groups_x), my))
-        for step in range(1, groups_x)
-    ]
-    for copy in rims:
-        copy.wait()
-    inner = short * (pairs + 1)
-
-    def fill_coarse(plane, main, left, right, slot, scale):
-        before = pltpu.roll(left, (128 - (pairs + slot) * short) % 128, 1) * at_y[0]
-        after = pltpu.roll(right, (inner - slot * short) % 128, 1) * at_y[1]
-        values = jnp.where(lane_full < short, before, main)
-        values = jnp.where(lane_full // short == pairs + 1, after, values)
-        coarse_padded[plane] = values * scale
-
-    for pair in range(pairs):
-        fill_coarse(pair + 1, pooled[pair], rim_in[0], rim_in[1], pair, 1.0)
-    fill_coarse(0, pooled_in[0], rim_corners_in[0, 0], rim_corners_in[0, 1], pairs - 1, at_x[0])
-    fill_coarse(pairs + 1, pooled_in[1], rim_corners_in[1, 0], rim_corners_in[1, 1], 0, at_x[1])
-    convolve(coarse_padded, coarse_ref[...], pairs, 128, 0, short)
-    point_high, point_low = split_pair(point_ref[...])
-    for pair in range(pairs):
-        high, low = split_pair(jax.nn.gelu(sums[pair + 2, :, 0:128]))
-        raised = dot(high, spread_ref[...]) + dot(low, spread_ref[...])
-        for x in (2 * pair, 2 * pair + 1):
-            joined = jnp.concatenate([fine[x] + raised, cells_ref[rows_of(x), :]], axis=0)
-            high, low = split_pair(joined)
-            value = dot(point_high, high) + dot(point_high, low) + dot(point_low, high)
-            base[rows_of(x), :] = value + bias_ref[...]
-    for copy in copies:
+    for copy in relays:
         copy.wait()
     load_weight.wait()
     lane = lax.broadcasted_iota(jnp.int32, (channels, lanes), 1)
@@ -374,21 +373,26 @@
             shift *= 2
         return picked
 
-    def along_x(own, others, rows, place):
+    def along_x(terms):
         first = jnp.zeros((channels, lanes), jnp.float32)
         second = jnp.zeros((channels, lanes), jnp.float32)
-        for step in range(groups_x):
-            base = lax.rem(mx - step + groups_x, groups_x) * rows
-            for row in range(rows):
-                position = place(base + row)
-                block = pl.ds(row * channels, channels)
-                values = own[block, :] if step == 0 else others[step, block, :]
-                first = first + values * table_x[position]
-                second = second + values * table_x[KX * total_x + position]
+        for values, position in terms:
+            first = first + values * table_x[position]
+            second = second + values * table_x[KX * total_x + position]
         return first, pltpu.roll(second, half, 1) * sign
 
+    def shifted(step):
+        return lax.rem(mx - step + groups_x, groups_x)
+
     def one_mode(j, carry):
-        first, second = along_x(line, line_in, cells_x, lambda x: (mx * rows_x + j) * total_x + x)
+        first, second = along_x(
+            (
+                lines[step] if hop == 0 else lines_in[hop, step],
+                (mx * rows_x + j) * total_x + shifted(hop) * cells_x + sources[step],
+            )
+            for hop in range(groups_x)
+            for step in range(groups_y)
+        )
         modes = first + second
         tiles = channels * KZ // lanes
         rows = [jnp.zeros((groups, lanes), jnp.float32) for _ in range(tiles)]
@@ -416,30 +420,77 @@
         send(2, step, mixed, mixed_in.at[step], (lax.rem(mx + step, groups_x), my))
         for step in range(1, groups_x)
     ]
+    for copy in rims:
+        copy.wait()
+    inner = short * (pairs + 1)
+
+    def fill_coarse(plane, main, left, right, slot, scale):
+        before = pltpu.roll(left, (128 - (pairs + slot) * short) % 128, 1) * at_y[0]
+        after = pltpu.roll(right, (inner - slot * short) % 128, 1) * at_y[1]
+        values = jnp.where(lane_full < short, before, main)
+        values = jnp.where(lane_full // short == pairs + 1, after, values)
+        coarse_padded[plane] = values * scale
+
+    for pair in range(pairs):
+        fill_coarse(pair + 1, pooled[pair], rim_in[0], rim_in[1], pair, 1.0)
+    fill_coarse(0, pooled_in[0], rim_corners_in[0, 0], rim_corners_in[0, 1], pairs - 1, at_x[0])
+    fill_coarse(pairs + 1, pooled_in[1], rim_corners_in[1, 0], rim_corners_in[1, 1], 0, at_x[1])
+    convolve(coarse_padded, coarse_ref[...], pairs, 128, 0, short)
+    point_high, point_low = split_pair(point_ref[...])
+    for pair in range(pairs):
+        high, low = split_pair(jax.nn.gelu(sums[pair + 2, :, 0:128]))
+        raised = dot(high, spread_ref[...]) + dot(low, spread_ref[...])
+        for x in (2 * pair, 2 * pair + 1):
+            joined = jnp.concatenate([fine[x] + raised, cells_ref[rows_of(x), :]], axis=0)
+            high, low = split_pair(joined)
+            value = dot(point_high, high) + dot(point_high, low) + dot(point_low, high)
+            base[rows_of(x), :] = value + bias_ref[...]
     for copy in copies:
         copy.wait()
 
-    def one_line(j, carry):
-        first, second = along_x(mixed, mixed_in, rows_x, lambda k: k * total_x + mx * cells_x + j)
-        back[pl.ds(pl.multiple_of(j * channels, channels), channels), :] = first - second
+    def one_line(step, carry):
+        place = mx * cells_x + lax.rem(my + step, groups_y)
+        first, second = along_x(
+            (
+                mixed[rows_of(row), :] if hop == 0 else mixed_in[hop, rows_of(row), :],
+                (shifted(hop) * rows_x + row) * total_x + place,
+            )
+            for hop in range(groups_x)
+            for row in range(rows_x)
+        )
+        back[step] = first - second
         return carry
 
-    lax.fori_loop(0, cells_x, one_line, 0)
-    copies = [
-        send(3, step, back, back_in.at[step], (mx, lax.rem(my + step, groups_y)))
+    lax.fori_loop(0, groups_y, one_line, 0)
+    copies = [None] + [
+        send(3, step, back.at[step], back_in.at[step], (mx, lax.rem(my + step, groups_y)))
         for step in range(1, groups_y)
     ]
     result = None
     for step in range(groups_y):
         if step:
-            copies[step - 1].wait()
-        values = back_in[step] if step else back[...]
-        peer = lax.rem(my - step + groups_y, groups_y)
-        turn = rotation[my * groups_y + peer]
-        values = values * turn[0:1] - pltpu.roll(values, half, 1) * turn[1:2]
-        term = dot_split(values, inv_high[peer], inv_low[peer])
+            copies[step].wait()
+        values = back_in[step] if step else back[0]
+        peer = sources[step]
+        rolled = pltpu.roll(values, half, 1)
+        turned = []
+        for tile in range(groups_y):
+            turn = rotation[lax.rem(my + tile, groups_y) * groups_y + peer]
+            turned.append(values * turn[0:1] - rolled * turn[1:2])
+        term = dot_split(jnp.concatenate(turned, axis=0), inv_high[peer], inv_low[peer])
         result = term if result is None else result + term
-    out_ref[...] = jax.nn.gelu(result + base[...])
+    for step in range(groups_y):
+        ready[step] = result[step * channels : (step + 1) * channels]
+    copies = [None] + [
+        send(4, step, ready.at[step], ready_in.at[step], (mx, lax.rem(my + step, groups_y)))
+        for step in range(1, groups_y)
+    ]
+    for step in range(groups_y):
+        if step:
+            copies[step].wait()
+        values = ready_in[step] if step else ready[0]
+        rows = aligned(sources[step])
+        out_ref[rows, :] = jax.nn.gelu(values + base[rows, :])
 
 
 def stacked(weight):
@@ -464,7 +515,7 @@
     groups_x, groups_y = lax.axis_size("gx"), lax.axis_size("gy")
     lanes = 2 * rows_y * KZ
     tables = spectral_tables(groups_x, groups_y, cells_x, cells_y, rows_y)
-    slab_x, slab_k = (cells_x * channels, lanes), (rows_x * channels, lanes)
+    slab_k = (rows_x * channels, lanes)
     f32 = jnp.float32
     vmem = pl.BlockSpec(memory_space=pltpu.VMEM)
     return pl.pallas_call(
@@ -477,17 +528,21 @@
         + [vmem] * 6,
         out_specs=vmem,
         scratch_shapes=[
-            pltpu.VMEM((groups_y, *slab_x), f32),
-            pltpu.VMEM((groups_y, *slab_x), f32),
-            pltpu.VMEM(slab_x, f32),
-            pltpu.VMEM((groups_x, *slab_x), f32),
+            pltpu.VMEM((groups_y, channels, plane), f32),
+            pltpu.VMEM((groups_y, channels, lanes), f32),
+            pltpu.VMEM((groups_y, channels, lanes), f32),
+            pltpu.VMEM((groups_x, groups_y, channels, lanes), f32),
             pltpu.VMEM(slab_k, f32),
             pltpu.VMEM((groups_x, *slab_k), f32),
-            pltpu.VMEM(slab_x, f32),
-            pltpu.VMEM((groups_y, *slab_x), f32),
+            pltpu.VMEM((groups_y, channels, lanes), f32),
+            pltpu.VMEM((groups_y, channels, lanes), f32),
+            pltpu.VMEM((groups_y, channels, plane), f32),
+            pltpu.VMEM((groups_y, channels, plane), f32),
             pltpu.VMEM(spectral_weight.shape, f32),
-            pltpu.SemaphoreType.DMA((4, max(groups_x, groups_y))),
-            pltpu.SemaphoreType.DMA((4, max(groups_x, groups_y))),
+            pltpu.SemaphoreType.DMA((5, max(groups_x, groups_y))),
+            pltpu.SemaphoreType.DMA((5, max(groups_x, groups_y))),
+            pltpu.SemaphoreType.DMA((groups_x, groups_y)),
+            pltpu.SemaphoreType.DMA((groups_x, groups_y)),
             pltpu.SemaphoreType.DMA,
             pltpu.VMEM((2, cells_x * NZ // 128, channels, 128), f32),
             pltpu.VMEM((2, cells_x * NZ // 128, channels, 128), f32),
@@ -576,7 +631,7 @@
         and plane % 128 == 0
         and cells_x % (128 // NZ) == 0
         and cells_x * NZ // 2 == 128
-        and cells_x == cells_y
+        and cells_x == cells_y == lax.axis_size("gy")
         and min(lax.axis_size("gx"), lax.axis_size("gy")) > 1
     ):
         out = layer(

time: 71.7 us -> 63.4 us (0.88)
  Pallas kernels: 64.5 us -> 56.1 us
    pallas_call x1, Pallas kernels: 64.5 us -> 56.1 us  [layer(): pl.pallas_call(functools.partial(spectral_kernel, groups_x, groups_y, cel...]
where the time goes in v2:
time: 63.4 us; the launch traced here: 63 us
  Pallas kernels  56.1 us (88%)
  local copies, waits for them, and re-layouts  6.69 us (11%)
    pallas_call x1, Pallas kernels, layer(): pl.pallas_call(functools.partial(spectral_kernel, groups_x, groups_y, cel...  56.1 us
    reshape x6, local copies, waits for them, and re-layouts, stacked(): weight.reshape(3, 9, outs, ins).transpose(0, 2, 1, 3)  3.41 us
    unnamed x26, local copies, waits for them, and re-layouts  2.25 us

profile of v2, /device:TPU:25, one launch (start us, length us, event | category | flops | bytes accessed | tf_op | source)
XLA Modules:
  0.0 63.0 jit_solution(13358341982496469117)
XLA Ops:
  0.0 0.0 copy-start.4
  0.0 0.0 copy-start.5
  0.0 0.0 copy-start.8
  0.0 0.0 copy-start.6
  0.1 0.0 copy-start.7
  0.1 0.0 copy-start.9
  0.1 0.0 copy-start.12
  0.1 0.0 copy-start.11
  0.1 0.0 copy-start.10
  0.1 1.4 %copy.22 = f32[3,9,32,32]{2,0,3,1:T(4,128)S(1)} copy(f32[3,9,32,32]{3,2,1,0:T(8,128)} %bitcast.19) | data formatting | bytes 221184 | tf_op jit(solution)/shard_map/reshape | solution.py:498
  1.5 0.2 reshape.20
  1.8 0.1 copy.24.fine_ref
  1.9 1.3 %copy.23 = f32[3,9,32,32]{2,0,3,1:T(4,128)S(1)} copy(f32[3,9,32,32]{3,2,1,0:T(8,128)} %bitcast.20) | data formatting | bytes 221184 | tf_op jit(solution)/shard_map/reshape | solution.py:498
  3.2 0.2 reshape.22
  3.4 0.1 copy.25.coarse_ref
  3.5 0.0 copy-done.9
  3.6 0.1 copy.21
  3.6 0.0 copy-done.12
  3.7 0.1 copy.26.bias_ref
  3.7 0.0 copy-done.11
  3.7 0.0 copy-done.10
  3.7 0.1 pad_maximum_fusion.point_ref
  3.8 0.0 copy-done.1
  3.8 0.0 copy-done.2
  3.8 0.0 copy-done.3
  3.8 0.0 copy-done.4
  3.8 0.0 copy-done.5
  3.9 0.0 copy-done.8
  3.9 0.0 copy-start
  3.9 2.2 %copy-done = f32[8,4,2,32,512]{4,3,2,1,0:T(8,128)S(1)} copy-done((f32[8,4,2,32,512]{4,3,2,1,0:T(8,128)S(1)}, f32[8,4,2,32,512]{4,3,2,1,0:T(8,128)}, u32[]{:S(2)}) %copy-start) | copy-done | bytes 4194328
  6.1 56.1 %shard_map.145 = f32[256,256]{1,0:T(8,128)S(1)} custom-call(f32[256,256]{1,0:T(8,128)S(1)} %bitcast.16, bf16[8,256,128]{2,1,0:T(8,128)(2,1)S(1)} %copy-done.1, bf16[8,256,128]{2,1,0:T(8,128)(2,1)S(1)} %copy-done.2, bf16[8,128,256]{2,1,0:T(8,128)(2,1)S(1)} %copy-done.3, bf16[8,128,256]{2,1,0:T(8,128)(2,1)S(1)} %copy-done.4, f32[64,2,128]{2,1,0:T(2,128)S(1)} %copy-done.5, ...), custom_call_target="tpu_custom_call" | custom-call | tf_op jit(solution)/shard_map/pallas_call | solution.py:521
  62.2 0.9 %copy.29 = f32[8,32,256]{2,0,1:T(8,128)} copy(f32[8,32,256]{2,1,0:T(8,128)S(1)} %bitcast.15) | data formatting | bytes 524288 | tf_op jit(solution)/shard_map/reshape | solution.py:641
  (5 shorter events, 0.0 us)
Async XLA Ops:
  0.0 3.8 %copy-start.1 = (bf16[8,256,128]{2,1,0:T(8,128)(2,1)S(1)}, bf16[8,256,128]{2,1,0:T(8,128)(2,1)}, u32[]{:S(2)}) copy-start(bf16[8,256,128]{2,1,0:T(8,128)(2,1)} %constant.16.clone.fwd_high) | copy-start | bytes 1572868
  0.0 3.8 %copy-start.2 = (bf16[8,256,128]{2,1,0:T(8,128)(2,1)S(1)}, bf16[8,256,128]{2,1,0:T(8,128)(2,1)}, u32[]{:S(2)}) copy-start(bf16[8,256,128]{2,1,0:T(8,128)(2,1)} %constant.17.clone.fwd_low) | copy-start | bytes 1572868
  0.0 3.8 %copy-start.3 = (bf16[8,128,256]{2,1,0:T(8,128)(2,1)S(1)}, bf16[8,128,256]{2,1,0:T(8,128)(2,1)}, u32[]{:S(2)}) copy-start(bf16[8,128,256]{2,1,0:T(8,128)(2,1)} %constant.18.clone.inv_high) | copy-start | bytes 1572868
  0.0 3.8 %copy-start.4 = (bf16[8,128,256]{2,1,0:T(8,128)(2,1)S(1)}, bf16[8,128,256]{2,1,0:T(8,128)(2,1)}, u32[]{:S(2)}) copy-start(bf16[8,128,256]{2,1,0:T(8,128)(2,1)} %constant.19.clone.inv_low) | copy-start | bytes 1572868
  0.0 3.8 %copy-start.5 = (f32[64,2,128]{2,1,0:T(2,128)S(1)}, f32[64,2,128]{2,1,0:T(2,128)}, u32[]{:S(2)}) copy-start(f32[64,2,128]{2,1,0:T(2,128)} %constant.20.clone.rotation) | copy-start | bytes 196612
  0.0 3.8 %copy-start.8 = (f32[2048]{0:T(1024)S(1)}, f32[2048]{0:T(1024)}, u32[]{:S(2)}) copy-start(f32[2048]{0:T(1024)} %constant.21.clone.table_x) | copy-start | bytes 24580
  0.0 3.8 %copy-start.6 = (bf16[256,128]{1,0:T(8,128)(2,1)S(1)}, bf16[256,128]{1,0:T(8,128)(2,1)}, u32[]{:S(2)}) copy-start(bf16[256,128]{1,0:T(8,128)(2,1)} %constant.22.clone.pool_ref) | copy-start | bytes 196612
  0.1 3.8 %copy-start.7 = (bf16[128,256]{1,0:T(8,128)(2,1)S(1)}, bf16[128,256]{1,0:T(8,128)(2,1)}, u32[]{:S(2)}) copy-start(bf16[128,256]{1,0:T(8,128)(2,1)} %constant.23.clone.spread_ref) | copy-start | bytes 196612
  0.1 3.5 %copy-start.9 = (f32[32,8,256]{2,1,0:T(8,128)S(1)}, f32[32,8,256]{2,1,0:T(8,128)}, u32[]{:S(2)}) copy-start(f32[32,8,256]{2,1,0:T(8,128)} %param.15) | copy-start | bytes 786436
  0.1 3.6 %copy-start.12 = (f32[32]{0:T(128)S(1)}, f32[32]{0:T(128)}, u32[]{:S(2)}) copy-start(f32[32]{0:T(128)} %param.21) | copy-start | bytes 388
  0.1 3.7 %copy-start.11 = (f32[32,32]{1,0:T(8,128)S(1)}, f32[32,32]{1,0:T(8,128)}, u32[]{:S(2)}) copy-start(f32[32,32]{1,0:T(8,128)} %param.19) | copy-start | bytes 12292
  0.1 3.6 %copy-start.10 = (f32[32,32]{1,0:T(8,128)S(1)}, f32[32,32]{1,0:T(8,128)}, u32[]{:S(2)}) copy-start(f32[32,32]{1,0:T(8,128)} %param.20) | copy-start | bytes 12292
  3.9 2.2 %copy-start = (f32[8,4,2,32,512]{4,3,2,1,0:T(8,128)S(1)}, f32[8,4,2,32,512]{4,3,2,1,0:T(8,128)}, u32[]{:S(2)}) copy-start(f32[8,4,2,32,512]{4,3,2,1,0:T(8,128)} %weight_hbm.1) | copy-start | bytes 12582916

commit v3 on v2

--- a/solution.py
+++ b/solution.py
@@ -148,20 +148,32 @@
 
 def spectral_kernel(
     groups_x, groups_y, cells_x, rows_x, rows_y, channels,
-    cells_ref, fwd_high, fwd_low, inv_high, inv_low, rotation, table_x, weight_hbm,
+    cells_ref, fwd_high_hbm, fwd_low_hbm, inv_high_hbm, inv_low_hbm, rotation, table_x, weight_hbm,
     fine_ref, coarse_ref, point_ref, bias_ref, pool_ref, spread_ref,
     out_ref,
     field_in, parts, lines, lines_in, mixed, mixed_in, back, back_in, ready, ready_in, weight,
     send_sem, recv_sem, relay_send, relay_recv, weight_sem,
     edges, edges_in, planes_in, corners_in, padded, stack_high, stack_low, sums, fine,
     pooled, rim, rim_in, pooled_in, rim_corners_in, coarse_padded, base,
-    halo_send, halo_recv,
+    halo_send, halo_recv, fwd_high, fwd_low, inv_high, inv_low, table_sem,
+    mixed_send, mixed_recv,
 ):
     mx, my = lax.axis_index("gx"), lax.axis_index("gy")
     lanes = 2 * rows_y * KZ
     groups = 2 * rows_y
     total_x = groups_x * cells_x
     load_weight = pltpu.make_async_copy(weight_hbm, weight, weight_sem)
+    loads = [
+        pltpu.make_async_copy(source, target, table_sem.at[index])
+        for index, (source, target) in enumerate(
+            (
+                (fwd_high_hbm, fwd_high), (fwd_low_hbm, fwd_low),
+                (inv_high_hbm, inv_high), (inv_low_hbm, inv_low),
+            )
+        )
+    ]
+    for load in loads:
+        load.start()
     load_weight.start()
     barrier = pltpu.get_barrier_semaphore()
     for step in range(1, groups_y):
@@ -243,6 +255,8 @@
     dot = functools.partial(jnp.dot, preferred_element_type=jnp.float32)
     for copy in fields:
         copy.wait()
+    loads[0].wait()
+    loads[1].wait()
     sources = [lax.rem(my - step + groups_y, groups_y) for step in range(groups_y)]
     stack = [cells_ref[aligned(my), :]] + [field_in[step] for step in range(1, groups_y)]
     left_high, left_low = split_pair(jnp.concatenate(stack, axis=0))
@@ -328,7 +342,7 @@
 
         lax.fori_loop(0, count + 2, one_plane, 0)
 
-    convolve(padded, fine_ref[...], cells_x, plane_lanes, 128, NZ)
+    convolve(padded, stacked(fine_ref), cells_x, plane_lanes, 128, NZ)
     pairs = cells_x // 2
     short = NZ // 2
     for x in range(cells_x):
@@ -383,6 +397,13 @@
 
     def shifted(step):
         return lax.rem(mx - step + groups_x, groups_x)
+
+    def mixed_copy(hop, j):
+        return pltpu.make_async_remote_copy(
+            src_ref=mixed.at[aligned(j), :], dst_ref=mixed_in.at[hop, aligned(j), :],
+            send_sem=mixed_send.at[hop, j], recv_sem=mixed_recv.at[hop, j],
+            device_id=(lax.rem(mx + hop, groups_x), my), device_id_type=MESH,
+        )
 
     def one_mode(j, carry):
         first, second = along_x(
@@ -413,13 +434,11 @@
                 turned = jnp.where(diagonal == d, moved, turned)
             start = pl.multiple_of(j * channels + tile * groups, groups)
             mixed[pl.ds(start, groups), :] = turned
+        for hop in range(1, groups_x):
+            mixed_copy(hop, j).start()
         return carry
 
     lax.fori_loop(0, rows_x, one_mode, 0)
-    copies = [
-        send(2, step, mixed, mixed_in.at[step], (lax.rem(mx + step, groups_x), my))
-        for step in range(1, groups_x)
-    ]
     for copy in rims:
         copy.wait()
     inner = short * (pairs + 1)
@@ -435,7 +454,7 @@
         fill_coarse(pair + 1, pooled[pair], rim_in[0], rim_in[1], pair, 1.0)
     fill_coarse(0, pooled_in[0], rim_corners_in[0, 0], rim_corners_in[0, 1], pairs - 1, at_x[0])
     fill_coarse(pairs + 1, pooled_in[1], rim_corners_in[1, 0], rim_corners_in[1, 1], 0, at_x[1])
-    convolve(coarse_padded, coarse_ref[...], pairs, 128, 0, short)
+    convolve(coarse_padded, stacked(coarse_ref), pairs, 128, 0, short)
     point_high, point_low = split_pair(point_ref[...])
     for pair in range(pairs):
         high, low = split_pair(jax.nn.gelu(sums[pair + 2, :, 0:128]))
@@ -445,8 +464,9 @@
             high, low = split_pair(joined)
             value = dot(point_high, high) + dot(point_high, low) + dot(point_low, high)
             base[rows_of(x), :] = value + bias_ref[...]
-    for copy in copies:
-        copy.wait()
+    for hop in range(1, groups_x):
+        for row in range(rows_x):
+            mixed_copy(hop, row).wait()
 
     def one_line(step, carry):
         place = mx * cells_x + lax.rem(my + step, groups_y)
@@ -466,6 +486,8 @@
         send(3, step, back.at[step], back_in.at[step], (mx, lax.rem(my + step, groups_y)))
         for step in range(1, groups_y)
     ]
+    loads[2].wait()
+    loads[3].wait()
     result = None
     for step in range(groups_y):
         if step:
@@ -494,8 +516,11 @@
 
 
 def stacked(weight):
-    taps, outs, ins = weight.shape
-    return weight.reshape(3, 9, outs, ins).transpose(0, 2, 1, 3).reshape(3 * outs, 9 * ins)
+    rows = [
+        jnp.concatenate([weight[9 * plane + tap] for tap in range(9)], axis=1)
+        for plane in range(3)
+    ]
+    return jnp.concatenate(rows, axis=0)
 
 
 def pooling(cells_y):
@@ -523,8 +548,10 @@
             spectral_kernel, groups_x, groups_y, cells_x, rows_x, rows_y, channels
         ),
         out_shape=jax.ShapeDtypeStruct((cells_x * channels, plane), f32),
-        in_specs=[vmem] * 6
-        + [pl.BlockSpec(memory_space=pltpu.SMEM), pl.BlockSpec(memory_space=pl.ANY)]
+        in_specs=[vmem]
+        + [pl.BlockSpec(memory_space=pltpu.HBM)] * 4
+        + [vmem]
+        + [pl.BlockSpec(memory_space=pltpu.SMEM), pl.BlockSpec(memory_space=pltpu.HBM)]
         + [vmem] * 6,
         out_specs=vmem,
         scratch_shapes=[
@@ -562,13 +589,17 @@
             pltpu.VMEM((cells_x * channels, plane), f32),
             pltpu.SemaphoreType.DMA((2, 8)),
             pltpu.SemaphoreType.DMA((2, 8)),
+            *(pltpu.VMEM(table.shape, jnp.bfloat16) for table in tables[:4]),
+            pltpu.SemaphoreType.DMA((4,)),
+            pltpu.SemaphoreType.DMA((groups_x, rows_x)),
+            pltpu.SemaphoreType.DMA((groups_x, rows_x)),
         ],
         compiler_params=pltpu.CompilerParams(
-            collective_id=0, has_side_effects=True, vmem_limit_bytes=32 * 1024 * 1024
+            collective_id=0, has_side_effects=True, vmem_limit_bytes=62 * 1024 * 1024
         ),
     )(
         cells.reshape(cells_x * channels, plane), *tables, spectral_weight,
-        stacked(conv_fine), stacked(conv_coarse),
+        conv_fine, conv_coarse,
         jnp.concatenate([conv_mix, linear_weight], axis=1), bias_vector[:, None],
         *pooling(cells_y),
     )

time: 63.4 us -> 62.4 us (0.984)
  the two profiles are of different devices: /device:TPU:25 before, /device:TPU:0 now
where the time goes in v3:
time: 62.4 us; the launch traced here: 62.1 us
  Pallas kernels  55.8 us (89%)
  local copies, waits for them, and re-layouts  4.88 us (8%)
  other arithmetic  1.41 us (2%)
    pallas_call x1, Pallas kernels, layer(): pl.pallas_call(functools.partial(spectral_kernel, groups_x, groups_y, cel...  55.8 us
    reshape x1, local copies, waits for them, and re-layouts, per_device(): return jnp.transpose(out.reshape(cells_x, channels, plane), (1, 0, 2))  1.81 us
    transpose x1, local copies, waits for them, and re-layouts, per_device(): jnp.transpose(state_field, (1, 0, 2))  1.74 us
    concatenate x1, other arithmetic, layer(): jnp.concatenate([conv_mix, linear_weight], axis=1)  1.41 us
    broadcast_in_dim x1, local copies, waits for them, and re-layouts, layer(): bias_vector[:, None]  1.33 us

profile of v3, /device:TPU:0, one launch (start us, length us, event | category | flops | bytes accessed | tf_op | source)
XLA Modules:
  0.0 62.1 jit_solution(5756206982884289180)
XLA Ops:
  0.0 1.4 %pad_maximum_fusion.point_ref = f32[32,64]{1,0:T(8,128)} fusion(f32[32,32]{1,0:T(8,128)} %param.20, f32[32,32]{1,0:T(8,128)} %param.19), kind=kLoop, calls=%fused_computation.1 | loop fusion | flops 2048 | bytes 16384 | tf_op jit(solution)/shard_map/concatenate | solution.py:603
  1.4 1.3 %copy.17.bias_ref = f32[32,1]{1,0:T(8,128)} copy(f32[32,1]{0,1:T(1,128)} %bitcast.10) | data formatting | bytes 256 | tf_op jit(solution)/shard_map/broadcast_in_dim | solution.py:603
  2.7 1.7 %copy.16 = f32[8,32,256]{2,1,0:T(8,128)} copy(f32[8,32,256]{2,0,1:T(8,128)} %bitcast.9) | data formatting | bytes 524288 | tf_op jit(solution)/shard_map/transpose | solution.py:669
  4.5 55.8 %shard_map.145 = f32[256,256]{1,0:T(8,128)} custom-call(f32[256,256]{1,0:T(8,128)} %bitcast.8, bf16[8,256,128]{2,1,0:T(8,128)(2,1)} %constant.16.clone.fwd_high_hbm, bf16[8,256,128]{2,1,0:T(8,128)(2,1)} %constant.17.clone.fwd_low_hbm, bf16[8,128,256]{2,1,0:T(8,128)(2,1)} %constant.18.clone.inv_high_hbm, bf16[8,128,256]{2,1,0:T(8,128)(2,1)} %constant.19.clone.inv_low_hbm, ...), custom_call_target="tpu_custom_call" | custom-call | tf_op jit(solution)/shard_map/pallas_call | solution.py:546
  60.3 1.8 %copy.20 = f32[8,32,256]{2,0,1:T(8,128)} copy(f32[8,32,256]{2,1,0:T(8,128)} %bitcast.7) | data formatting | bytes 524288 | tf_op jit(solution)/shard_map/reshape | solution.py:672

commit v4 on v3

--- a/solution.py
+++ b/solution.py
@@ -148,15 +148,15 @@
 
 def spectral_kernel(
     groups_x, groups_y, cells_x, rows_x, rows_y, channels,
-    cells_ref, fwd_high_hbm, fwd_low_hbm, inv_high_hbm, inv_low_hbm, rotation, table_x, weight_hbm,
-    fine_ref, coarse_ref, point_ref, bias_ref, pool_ref, spread_ref,
+    state_ref, fwd_high_hbm, fwd_low_hbm, inv_high_hbm, inv_low_hbm, rotation, table_x, weight_hbm,
+    fine_ref, coarse_ref, mix_ref, linear_ref, bias_ref, pool_ref, spread_ref,
     out_ref,
     field_in, parts, lines, lines_in, mixed, mixed_in, back, back_in, ready, ready_in, weight,
     send_sem, recv_sem, relay_send, relay_recv, weight_sem,
     edges, edges_in, planes_in, corners_in, padded, stack_high, stack_low, sums, fine,
     pooled, rim, rim_in, pooled_in, rim_corners_in, coarse_padded, base,
     halo_send, halo_recv, fwd_high, fwd_low, inv_high, inv_low, table_sem,
-    mixed_send, mixed_recv,
+    mixed_send, mixed_recv, cells_ref,
 ):
     mx, my = lax.axis_index("gx"), lax.axis_index("gy")
     lanes = 2 * rows_y * KZ
@@ -175,6 +175,8 @@
     for load in loads:
         load.start()
     load_weight.start()
+    for x in range(cells_x):
+        cells_ref[x * channels : (x + 1) * channels, :] = state_ref[:, x, :]
     barrier = pltpu.get_barrier_semaphore()
     for step in range(1, groups_y):
         pl.semaphore_signal(
@@ -455,7 +457,10 @@
     fill_coarse(0, pooled_in[0], rim_corners_in[0, 0], rim_corners_in[0, 1], pairs - 1, at_x[0])
     fill_coarse(pairs + 1, pooled_in[1], rim_corners_in[1, 0], rim_corners_in[1, 1], 0, at_x[1])
     convolve(coarse_padded, stacked(coarse_ref), pairs, 128, 0, short)
-    point_high, point_low = split_pair(point_ref[...])
+    point_high, point_low = split_pair(jnp.concatenate([mix_ref[...], linear_ref[...]], axis=1))
+    across = lax.broadcasted_iota(jnp.int32, (channels, channels), 0)
+    along = lax.broadcasted_iota(jnp.int32, (channels, channels), 1)
+    bias = jnp.sum(jnp.where(across == along, bias_ref[...], 0.0), axis=1, keepdims=True)
     for pair in range(pairs):
         high, low = split_pair(jax.nn.gelu(sums[pair + 2, :, 0:128]))
         raised = dot(high, spread_ref[...]) + dot(low, spread_ref[...])
@@ -463,7 +468,7 @@
             joined = jnp.concatenate([fine[x] + raised, cells_ref[rows_of(x), :]], axis=0)
             high, low = split_pair(joined)
             value = dot(point_high, high) + dot(point_high, low) + dot(point_low, high)
-            base[rows_of(x), :] = value + bias_ref[...]
+            base[rows_of(x), :] = value + bias
     for hop in range(1, groups_x):
         for row in range(rows_x):
             mixed_copy(hop, row).wait()
@@ -535,7 +540,7 @@
 def layer(
     cells, spectral_weight, conv_fine, conv_coarse, conv_mix, linear_weight, bias_vector, cells_y
 ):
-    cells_x, channels, plane = cells.shape
+    channels, cells_x, plane = cells.shape
     rows_x, rows_y = spectral_weight.shape[:2]
     groups_x, groups_y = lax.axis_size("gx"), lax.axis_size("gy")
     lanes = 2 * rows_y * KZ
@@ -552,7 +557,7 @@
         + [pl.BlockSpec(memory_space=pltpu.HBM)] * 4
         + [vmem]
         + [pl.BlockSpec(memory_space=pltpu.SMEM), pl.BlockSpec(memory_space=pltpu.HBM)]
-        + [vmem] * 6,
+        + [vmem] * 7,
         out_specs=vmem,
         scratch_shapes=[
             pltpu.VMEM((groups_y, channels, plane), f32),
@@ -593,14 +598,15 @@
             pltpu.SemaphoreType.DMA((4,)),
             pltpu.SemaphoreType.DMA((groups_x, rows_x)),
             pltpu.SemaphoreType.DMA((groups_x, rows_x)),
+            pltpu.VMEM((cells_x * channels, plane), f32),
         ],
         compiler_params=pltpu.CompilerParams(
             collective_id=0, has_side_effects=True, vmem_limit_bytes=62 * 1024 * 1024
         ),
     )(
-        cells.reshape(cells_x * channels, plane), *tables, spectral_weight,
+        cells, *tables, spectral_weight,
         conv_fine, conv_coarse,
-        jnp.concatenate([conv_mix, linear_weight], axis=1), bias_vector[:, None],
+        conv_mix, linear_weight, bias_vector.reshape(1, channels),
         *pooling(cells_y),
     )
 
@@ -666,7 +672,7 @@
         and min(lax.axis_size("gx"), lax.axis_size("gy")) > 1
     ):
         out = layer(
-            jnp.transpose(state_field, (1, 0, 2)), spectral_weight, conv_fine, conv_coarse,
+            state_field, spectral_weight, conv_fine, conv_coarse,
             conv_mix, linear_weight, bias_vector, cells_y,
         )
         return jnp.transpose(out.reshape(cells_x, channels, plane), (1, 0, 2))

time: 62.4 us -> 57.9 us (0.928)
  local copies, waits for them, and re-layouts: 4.88 us -> 1.81 us
  other arithmetic: 1.41 us -> 0 us
    transpose x1 -> x0, local copies, waits for them, and re-layouts: 1.74 us -> none  [per_device(): jnp.transpose(state_field, (1, 0, 2))]
    concatenate x1 -> x0, other arithmetic: 1.41 us -> none  [layer(): jnp.concatenate([conv_mix, linear_weight], axis=1)]
    broadcast_in_dim x1 -> x0, local copies, waits for them, and re-layouts: 1.33 us -> none  [layer(): bias_vector[:, None]]
where the time goes in v4:
time: 57.9 us; the launch traced here: 57.7 us
  Pallas kernels  55.9 us (97%)
  local copies, waits for them, and re-layouts  1.81 us (3%)
    pallas_call x1, Pallas kernels, layer(): pl.pallas_call(functools.partial(spectral_kernel, groups_x, groups_y, cel...  55.9 us
    reshape x1, local copies, waits for them, and re-layouts, per_device(): return jnp.transpose(out.reshape(cells_x, channels, plane), (1, 0, 2))  1.81 us

profile of v4, /device:TPU:0, one launch (start us, length us, event | category | flops | bytes accessed | tf_op | source)
XLA Modules:
  0.0 57.7 jit_solution(14433090998015638871)
XLA Ops:
  0.0 55.9 %shard_map.145 = f32[256,256]{1,0:T(8,128)} custom-call(f32[32,8,256]{2,1,0:T(8,128)} %state_ref.1, bf16[8,256,128]{2,1,0:T(8,128)(2,1)} %constant.16.clone.fwd_high_hbm, bf16[8,256,128]{2,1,0:T(8,128)(2,1)} %constant.17.clone.fwd_low_hbm, bf16[8,128,256]{2,1,0:T(8,128)(2,1)} %constant.18.clone.inv_high_hbm, ...), custom_call_target="tpu_custom_call" | custom-call | tf_op jit(solution)/shard_map/pallas_call | solution.py:551
  55.9 1.8 %copy.18 = f32[8,32,256]{2,0,1:T(8,128)} copy(f32[8,32,256]{2,1,0:T(8,128)} %bitcast.5) | data formatting | bytes 524288 | tf_op jit(solution)/shard_map/reshape | solution.py:678
